TPU v7x, 32 devices: a whole 2x2x4 slice. The times are simulated.
32 devices in a mesh: dp: 4 (over x, core), expert: 8 (over z, y).
Axes of the slice: x: 2, y: 2, z: 4, core: 2. Of those that a mesh axis runs over, the one named last changes fastest.
Arguments:
- tokens: bfloat16 [16384, 768], P(('dp', 'expert')), may hold values from -6 to 6
- cotangent: bfloat16 [16384, 768], P(('dp', 'expert')), may hold values from -6 to 6
- chosen: int32 [16384, 2], P(('dp', 'expert')), may hold values from 0 to 9, all different within a row; in each aligned block of 512 rows (0 to 511, 512 to 1023, ...) at most 128 rows name the same one
- gates: float32 [16384, 2], P(('dp', 'expert')), may hold values from 0.2 to 0.8
- lengths: int32 [32, 8], P(('dp', 'expert')), may hold values from 1 to 256, 512 in all within a row
- keep_mask: int32 [16384], P(('dp', 'expert')), may hold values 0 or 1
- gain1: float32 [768], replicated, may hold values from 0.5 to 1.5
- w_qkv: bfloat16 [768, 2304], replicated, may hold values from -0.21875 to 0.21875
- w_o: bfloat16 [768, 768], replicated, may hold values from -0.875 to 0.875
- gain2: float32 [768], replicated, may hold values from 0.5 to 1.5
- frozen_in: bfloat16 [2, 3072, 768], replicated, may hold values from -0.21875 to 0.21875
- frozen_out: bfloat16 [2, 3072, 768], replicated, may hold values from -0.109375 to 0.109375
- w_in: bfloat16 [8, 3072, 768], P('expert', 'dp'), may hold values from -0.21875 to 0.21875
- w_out: bfloat16 [8, 3072, 768], P('expert', 'dp'), may hold values from -0.109375 to 0.109375
Outputs:
- output: bfloat16 [16384, 768], P(('dp', 'expert'))
- d_tokens: bfloat16 [16384, 768], P(('dp', 'expert'))
- d_gain1: float32 [768], replicated
- d_w_qkv: float32 [768, 2304], replicated
- d_w_o: float32 [768, 768], replicated
- d_gain2: float32 [768], replicated
- d_w_in: float32 [8, 3072, 768], P('expert', 'dp')
- d_w_out: float32 [8, 3072, 768], P('expert', 'dp')
- counts: float32 [10], replicated
Inputs may be any that keep to these rules, and one draw needn't show every extreme that they name: `chosen`: each token names two different experts; among the 512 tokens of one device no expert is named more than 128 times, a bound that some block reaches. The 8 lengths of a device sum to 512; the longest is exactly 256.
All inputs are finite; a program needn't handle non-finite values. No bound on the sum of `keep_mask` on one device may be relied on, other than what follows from the above.
Results may differ from a plain program's by a relative error of at most 0.012.
Values may be sent and summed in bfloat16 or wider, within the bound.
A program may use at most 256 MiB of HBM per device.

v0:
```python
import jax
import jax.numpy as jnp
from jax import lax
from jax.sharding import PartitionSpec as P

HEADS = 12
HEAD_DIM = 64
FROZEN = 2


def layer_norm(values_in, gain_vec):
    row_mean = jnp.mean(values_in, axis=-1, keepdims=True)
    centred = values_in - row_mean
    variance = jnp.mean(centred * centred, axis=-1, keepdims=True)
    return centred * lax.rsqrt(variance + 1e-05) * gain_vec


def expert_forward(rows_low, up_weights, down_weights):
    hidden = jnp.einsum("gcd,gfd->gcf", rows_low, up_weights, preferred_element_type=jnp.float32)
    active = jax.nn.gelu(hidden).astype(jnp.bfloat16)
    result_rows = jnp.einsum(
        "gcf,gfd->gcd", active, down_weights, preferred_element_type=jnp.float32
    ).astype(jnp.bfloat16)
    return (result_rows, hidden)


def expert_backward(result_grad, hidden, up_weights, down_weights):
    active_grad = jnp.einsum(
        "gcd,gfd->gcf", result_grad, down_weights, preferred_element_type=jnp.float32
    )
    active, gelu_back = jax.vjp(jax.nn.gelu, hidden)
    hidden_grad = gelu_back(active_grad)[0].astype(jnp.bfloat16)
    input_grad = jnp.einsum(
        "gcf,gfd->gcd", hidden_grad, up_weights, preferred_element_type=jnp.float32
    ).astype(jnp.bfloat16)
    return (input_grad, hidden_grad, active.astype(jnp.bfloat16))


def block_scores(query_part, key_heads, allowed):
    scores = (
        jnp.einsum("qhd,khd->hqk", query_part, key_heads, preferred_element_type=jnp.float32)
        * 0.125
    )
    return jnp.where(allowed[None], scores, -1e30)


def body(
    tokens,
    cotangent,
    chosen,
    gates,
    lengths,
    keep_mask,
    gain1,
    w_qkv,
    w_o,
    gain2,
    frozen_in,
    frozen_out,
    w_in,
    w_out,
):
    row_count = tokens.shape[0]
    feat_width = tokens.shape[1]
    owners = lax.axis_size("expert")
    kind_count = FROZEN + owners
    slot_count = (2 * row_count * 5 // (4 * kind_count) + 7) // 8 * 8
    block_rows = min(512, row_count)
    weights_in, weights_out = (
        lax.all_gather(w_in, "dp", axis=1, tiled=True),
        lax.all_gather(w_out, "dp", axis=1, tiled=True),
    )
    tokens_full = tokens.astype(jnp.float32)
    normed_one, norm_one_back = jax.vjp(layer_norm, tokens_full, gain1)
    normed_one_low = normed_one.astype(jnp.bfloat16)
    projected = jnp.dot(normed_one_low, w_qkv, preferred_element_type=jnp.float32).astype(
        jnp.bfloat16
    )
    queries = projected[:, :feat_width].reshape(row_count, HEADS, HEAD_DIM)
    key_heads = projected[:, feat_width : 2 * feat_width].reshape(row_count, HEADS, HEAD_DIM)
    value_heads = projected[:, 2 * feat_width :].reshape(row_count, HEADS, HEAD_DIM)
    places = jnp.arange(row_count, dtype=jnp.int32)
    doc_ends = jnp.cumsum(lengths[0])
    documents = jnp.sum((places[:, None] >= doc_ends[None, :]).astype(jnp.int32), axis=1)

    def permitted():
        return (
            (documents[:, None] == documents[None, :])
            & (places[None, :] <= places[:, None])
            & ((keep_mask[None, :] > 0) | (places[None, :] == places[:, None]))
        )

    scores = block_scores(queries, key_heads, permitted())
    peak_score = jnp.max(scores, axis=-1, keepdims=True)
    exp_scores = jnp.exp(scores - peak_score)
    exp_total = jnp.sum(exp_scores, axis=-1, keepdims=True)
    probs_low = (exp_scores / exp_total).astype(jnp.bfloat16)
    block_out = jnp.einsum(
        "hqk,khd->qhd", probs_low, value_heads, preferred_element_type=jnp.float32
    )
    out_blocks = block_out.reshape(block_rows, feat_width).astype(jnp.bfloat16)
    lse_blocks = [peak_score + jnp.log(exp_total)]
    mixed_rows = tokens_full + jnp.dot(out_blocks, w_o, preferred_element_type=jnp.float32)
    normed_two, norm_two_back = jax.vjp(layer_norm, mixed_rows, gain2)
    normed_two_low = normed_two.astype(jnp.bfloat16)
    flat_ids = chosen.reshape(-1)
    one_hot = (flat_ids[:, None] == jnp.arange(kind_count, dtype=jnp.int32)[None, :]).astype(
        jnp.int32
    )
    slot_ranks = jnp.sum(jnp.cumsum(one_hot, axis=0) * one_hot, axis=1) - 1
    positions = flat_ids * slot_count + slot_ranks
    buffer_rows = (
        jnp.zeros((kind_count * slot_count, feat_width), jnp.bfloat16)
        .at[positions]
        .set(jnp.repeat(normed_two_low, 2, axis=0))
    )
    local_rows = buffer_rows[: FROZEN * slot_count].reshape(FROZEN, slot_count, feat_width)
    routed_rows = buffer_rows[FROZEN * slot_count :].reshape(owners, slot_count, feat_width)
    arrived_rows = lax.all_to_all(routed_rows, "expert", split_axis=0, concat_axis=0, tiled=True)
    result_rows, _ = expert_forward(
        arrived_rows.reshape(1, -1, feat_width), weights_in, weights_out
    )
    served = result_rows.reshape(arrived_rows.shape)
    frozen_result, frozen_hidden = expert_forward(local_rows, frozen_in, frozen_out)
    returned = lax.all_to_all(served, "expert", split_axis=0, concat_axis=0, tiled=True)
    results = jnp.concatenate(
        [frozen_result.reshape(-1, feat_width), returned.reshape(-1, feat_width)], axis=0
    )
    picked = results[positions].astype(jnp.float32).reshape(row_count, 2, feat_width)
    output = mixed_rows + jnp.sum(picked * gates[:, :, None], axis=1)
    grad_out = cotangent.astype(jnp.float32)
    weighted = (jnp.repeat(grad_out, 2, axis=0) * gates.reshape(-1, 1)).astype(jnp.bfloat16)
    grad_buffer = (
        jnp.zeros((kind_count * slot_count, feat_width), jnp.bfloat16).at[positions].set(weighted)
    )
    frozen_grad_rows = grad_buffer[: FROZEN * slot_count].reshape(FROZEN, slot_count, feat_width)
    routed_grad = grad_buffer[FROZEN * slot_count :].reshape(owners, slot_count, feat_width)
    arrived_grad = lax.all_to_all(routed_grad, "expert", split_axis=0, concat_axis=0, tiled=True)
    flat_rows = arrived_rows.reshape(1, -1, feat_width)
    flat_grad = arrived_grad.reshape(1, -1, feat_width)
    hidden_all = jnp.einsum(
        "gcd,gfd->gcf", flat_rows, weights_in, preferred_element_type=jnp.float32
    )
    row_input_grad, hidden_grad, active = expert_backward(
        flat_grad, hidden_all, weights_in, weights_out
    )
    sent_back = lax.all_to_all(
        row_input_grad.reshape(owners, slot_count, feat_width),
        "expert",
        split_axis=0,
        concat_axis=0,
        tiled=True,
    )
    frozen_input_grad, _, _ = expert_backward(
        frozen_grad_rows, frozen_hidden, frozen_in, frozen_out
    )
    hidden_rows = hidden_grad[0]
    active_rows = active[0]
    input_rows = flat_rows[0]
    output_rows = flat_grad[0]
    term_in = lax.dot_general(
        hidden_rows, input_rows, (((0,), (0,)), ((), ())), preferred_element_type=jnp.float32
    )
    term_out = lax.dot_general(
        active_rows, output_rows, (((0,), (0,)), ((), ())), preferred_element_type=jnp.float32
    )
    summed = lax.psum_scatter(
        jnp.concatenate([term_in, term_out], axis=1), "dp", scatter_dimension=0, tiled=True
    )
    d_w_in = summed[:, :feat_width][None]
    d_w_out = summed[:, feat_width:][None]
    row_grads = jnp.concatenate(
        [frozen_input_grad.reshape(-1, feat_width), sent_back.reshape(-1, feat_width)], axis=0
    )
    normed_two_grad = jnp.sum(
        row_grads[positions].astype(jnp.float32).reshape(row_count, 2, feat_width), axis=1
    )
    mixed_part, gain2_grad = norm_two_back(normed_two_grad)
    mixed_grad = grad_out + mixed_part
    branch_grad = mixed_grad.astype(jnp.bfloat16)
    w_o_grad = lax.dot_general(
        out_blocks, branch_grad, (((0,), (0,)), ((), ())), preferred_element_type=jnp.float32
    )
    attended_grad = lax.dot_general(
        branch_grad, w_o, (((1,), (1,)), ((), ())), preferred_element_type=jnp.float32
    ).astype(jnp.bfloat16)
    attended_heads = attended_grad.reshape(row_count, HEADS, HEAD_DIM)
    key_grad = jnp.zeros((row_count, HEADS, HEAD_DIM), jnp.float32)
    value_grad = jnp.zeros((row_count, HEADS, HEAD_DIM), jnp.float32)
    query_grads = []
    for block_index, row_start in enumerate(range(0, row_count, block_rows)):
        scores = block_scores(queries, key_heads, permitted())
        probs_full = jnp.exp(scores - lse_blocks[block_index])
        probs_low = probs_full.astype(jnp.bfloat16)
        prob_grad = jnp.einsum(
            "qhd,khd->hqk", attended_heads, value_heads, preferred_element_type=jnp.float32
        )
        row_delta = jnp.sum(probs_full * prob_grad, axis=-1, keepdims=True)
        score_grad = (probs_full * (prob_grad - row_delta)).astype(jnp.bfloat16)
        query_grads.append(
            jnp.einsum("hqk,khd->qhd", score_grad, key_heads, preferred_element_type=jnp.float32)
            * 0.125
        )
        key_grad = (
            jnp.einsum("hqk,qhd->khd", score_grad, queries, preferred_element_type=jnp.float32)
            * 0.125
        )
        value_grad = jnp.einsum(
            "hqk,qhd->khd", probs_low, attended_heads, preferred_element_type=jnp.float32
        )
    projected_grad = jnp.concatenate(
        [
            query_grads[0].reshape(row_count, feat_width),
            key_grad.reshape(row_count, feat_width),
            value_grad.reshape(row_count, feat_width),
        ],
        axis=1,
    ).astype(jnp.bfloat16)
    w_qkv_grad = lax.dot_general(
        normed_one_low, projected_grad, (((0,), (0,)), ((), ())), preferred_element_type=jnp.float32
    )
    normed_one_grad = lax.dot_general(
        projected_grad, w_qkv, (((1,), (1,)), ((), ())), preferred_element_type=jnp.float32
    )
    tokens_part, gain1_grad = norm_one_back(normed_one_grad)
    tokens_grad = (mixed_grad + tokens_part).astype(jnp.bfloat16)
    local_counts = jnp.sum(one_hot, axis=0).astype(jnp.float32)
    gain1_sum, w_qkv_sum, w_o_sum, gain2_sum, counts = lax.psum(
        (gain1_grad, w_qkv_grad, w_o_grad, gain2_grad, local_counts), ("dp", "expert")
    )
    return (
        output.astype(jnp.bfloat16),
        tokens_grad,
        gain1_sum,
        w_qkv_sum,
        w_o_sum,
        gain2_sum,
        d_w_in,
        d_w_out,
        counts,
    )


def solution(mesh):
    placed = (
        P(("dp", "expert"), None),
        P(("dp", "expert"), None),
        P(("dp", "expert"), None),
        P(("dp", "expert"), None),
        P(("dp", "expert"), None),
        P(("dp", "expert")),
        P(),
        P(),
        P(),
        P(),
        P(),
        P(),
        P("expert", "dp", None),
        P("expert", "dp", None),
    )
    return jax.shard_map(
        body,
        mesh=mesh,
        in_specs=placed,
        out_specs=(
            P(("dp", "expert"), None),
            P(("dp", "expert"), None),
            P(),
            P(),
            P(),
            P(),
            P("expert", "dp", None),
            P("expert", "dp", None),
            P(),
        ),
        check_vma=False,
    )
```

profile of v0, /device:TPU:0, one launch (start us, length us, event | category | flops | bytes accessed | tf_op | source)
XLA Modules:
  0.0 601.9 jit_solution(12574793378495375460)
XLA Ops:
  14.4 6.2 %reduce-window.19 = s32[10,8,128]{2,1,0:T(8,128)} reduce-window(s32[10,8,128]{2,1,0:T(8,128)} %fusion.76, s32[]{:T(128)} %constant.21.clone.1), window={size=1x1x128 pad=0_0x0_0x127_0}, to_apply=%region_6.7 | reduce-window | flops 1300480 | bytes 81924 | tf_op jit(solution)/shard_map/reduce-window.1
  55.7 5.4 fusion.59
  72.2 7.2 %scatter_custom_fusion = bf16[1280,768]{1,0:T(8,128)(2,1)} fusion(s32[1024]{0:T(1024)S(1)} %bitcast.116, bf16[1024,768]{1,0:T(8,128)(2,1)} %reshape.407, bf16[]{:T(256)} %constant.25.clone.1), kind=kCustom, calls=%fused_computation.98 | custom fusion | bytes 1966592 | tf_op jit(solution)/shard_map/scatter | solution.py:115
  82.1 7.3 %all-to-all-start = ((bf16[8,128,768]{2,1,0:T(8,128)(2,1)}), bf16[8,128,768]{2,1,0:T(8,128)(2,1)}, u32[]{:S(2)}, u32[]{:S(2)}) async-start(bf16[8,128,768]{2,1,0:T(8,128)(2,1)} %bitcast.96), calls=%async_computation | async-start | bytes 3145728 | tf_op jit(solution)/shard_map/all_to_all | solution.py:119
  95.7 5.4 reshape.374
  101.1 8.1 %scatter_custom_fusion.1 = bf16[1280,768]{1,0:T(8,128)(2,1)} fusion(s32[1024]{0:T(1024)S(1)} %bitcast.117, f32[1024,768]{1,0:T(8,128)} %reshape.374, f32[1024]{0:T(1024)S(1)} %mul.298, bf16[]{:T(256)} %constant.25.clone.1), kind=kCustom, calls=%fused_computation.71 | custom fusion | flops 1572864 | bytes 5115906 | tf_op jit(solution)/shard_map/scatter | solution.py:134
  111.8 14.8 %all-to-all-done = bf16[8,128,768]{2,1,0:T(8,128)(2,1)} async-done(((bf16[8,128,768]{2,1,0:T(8,128)(2,1)}), bf16[8,128,768]{2,1,0:T(8,128)(2,1)}, u32[]{:S(2)}, u32[]{:S(2)}) %all-to-all-start) | async-done | bytes 1572896 | tf_op jit(solution)/shard_map/all_to_all | solution.py:119
  130.9 10.3 %fusion.19 = f32[1024,3072]{1,0:T(8,128)} fusion(bf16[1024,768]{1,0:T(8,128)(2,1)} %bitcast.14, bf16[1,3072,768]{2,1,0:T(8,128)(2,1)} %all-gather.3.cloned.1.call-done), kind=kOutput, calls=%fused_computation.32 | convolution fusion | flops 4831838208 | bytes 18874368 | tf_op jit(solution)/shard_map/gcd,gfd->gcf/dot_general | solution.py:19
  141.2 26.3 %all-to-all-done.2 = bf16[8,128,768]{2,1,0:T(8,128)(2,1)} async-done(((bf16[8,128,768]{2,1,0:T(8,128)(2,1)}), bf16[8,128,768]{2,1,0:T(8,128)(2,1)}, u32[]{:S(2)}, u32[]{:S(2)}) %all-to-all-start.2) | async-done | bytes 1572896 | tf_op jit(solution)/shard_map/all_to_all | solution.py:138
  167.5 11.3 %fusion.98 = f32[3072,768]{0,1:T(8,128)} fusion(bf16[1024,768]{1,0:T(8,128)(2,1)} %bitcast.22, f32[1024,3072]{1,0:T(8,128)} %fusion.19), kind=kOutput, calls=%fused_computation.147 | convolution fusion | flops 4860149760 | bytes 23592960 | tf_op jit(solution)/shard_map/dot_general | solution.py:164
  178.8 15.5 %fusion.6 = bf16[1024,3072]{1,0:T(8,128)(2,1)S(1)} fusion(f32[1024,3072]{1,0:T(8,128)} %fusion.19, bf16[1024,768]{1,0:T(8,128)(2,1)} %bitcast.22, bf16[1,3072,768]{2,1,0:T(8,128)(2,1)} %all-gather.5.cloned.1.call-done), kind=kOutput, calls=%fused_computation.13 | convolution fusion | flops 4894752768 | bytes 25165824 | tf_op jit(solution)/shard_map/gcd,gfd->gcf/dot_general | solution.py:28
  194.4 8.3 %fusion.105 = f32[3072,768]{0,1:T(8,128)S(1)} fusion(bf16[1024,3072]{1,0:T(8,128)(2,1)S(1)} %fusion.6, bf16[1024,768]{1,0:T(8,128)(2,1)} %bitcast.14), kind=kOutput, calls=%fused_computation.153 | convolution fusion | flops 4831838208 | bytes 17301504 | tf_op jit(solution)/shard_map/dot_general | solution.py:161
  202.7 6.9 %pad_maximum_fusion = f32[3072,1536]{0,1:T(8,128)} fusion(f32[3072,768]{0,1:T(8,128)S(1)} %copy-done.11, f32[3072,768]{0,1:T(8,128)S(1)} %fusion.105), kind=kLoop, calls=%fused_computation.4 | loop fusion | flops 4718592 | bytes 37748736 | tf_op jit(solution)/shard_map/concatenate | solution.py:168
  209.6 12.5 %fusion.40 = bf16[1024,768]{1,0:T(8,128)(2,1)} fusion(bf16[1,3072,768]{2,1,0:T(8,128)(2,1)} %all-gather.5.cloned.1.call-done, f32[1024,3072]{1,0:T(8,128)} %fusion.19), kind=kOutput, calls=%fused_computation.65 | convolution fusion | flops 4860936192 | bytes 18874368 | tf_op jit(solution)/shard_map/gcf,gfd->gcd/dot_general | solution.py:21
  229.8 8.8 %fusion.104 = f32[2,128,3072]{2,1,0:T(8,128)S(1)} fusion(bf16[2,128,768]{2,1,0:T(8,128)(2,1)S(1)} %bitcast.104, bf16[2,3072,768]{2,1,0:T(8,128)(2,1)} %param.24), kind=kOutput, calls=%fused_computation.152 | convolution fusion | flops 1207959552 | bytes 12976128 | tf_op jit(solution)/shard_map/gcd,gfd->gcf/dot_general | solution.py:19
  238.7 7.5 %fusion.63 = bf16[2,128,768]{2,1,0:T(8,128)(2,1)} fusion(bf16[2,3072,768]{2,1,0:T(8,128)(2,1)} %param.25, f32[2,128,3072]{2,1,0:T(8,128)S(1)} %fusion.104), kind=kOutput, calls=%fused_computation.91 | convolution fusion | flops 1215234048 | bytes 12976128 | tf_op jit(solution)/shard_map/gcf,gfd->gcd/dot_general | solution.py:21
  246.2 6.1 %fusion.37 = bf16[1024,768]{1,0:T(8,128)(2,1)} fusion(bf16[1024,3072]{1,0:T(8,128)(2,1)S(1)} %bitcast.128, bf16[1,3072,768]{2,1,0:T(8,128)(2,1)S(1)} %bitcast.123), kind=kOutput, calls=%fused_computation.64 | convolution fusion | flops 4832624640 | bytes 12582912 | tf_op jit(solution)/shard_map/gcf,gfd->gcd/dot_general | solution.py:33
  252.4 11.1 %all-to-all-done.1 = bf16[8,128,768]{2,1,0:T(8,128)(2,1)} async-done(((bf16[8,128,768]{2,1,0:T(8,128)(2,1)}), bf16[8,128,768]{2,1,0:T(8,128)(2,1)}, u32[]{:S(2)}, u32[]{:S(2)}) %all-to-all-start.1) | async-done | bytes 1572896 | tf_op jit(solution)/shard_map/all_to_all | solution.py:125
  269.3 13.3 %fusion.60 = bf16[2,128,768]{2,1,0:T(8,128)(2,1)} fusion(bf16[2,3072,768]{2,1,0:T(8,128)(2,1)} %param.24, f32[2,128,3072]{2,1,0:T(8,128)} %copy-done.19, bf16[2,128,768]{2,1,0:T(8,128)(2,1)} %bitcast.111, bf16[2,3072,768]{2,1,0:T(8,128)(2,1)} %param.25), kind=kOutput, calls=%fused_computation.90 | convolution fusion | flops 2431844352 | bytes 22806528 | tf_op jit(solution)/shard_map/gcf,gfd->gcd/dot_general | solution.py:33
  285.4 7.6 %gather_fusion = bf16[1024,768]{1,0:T(8,128)(2,1)} fusion(bf16[1280,768]{1,0:T(8,128)(2,1)} %pad_maximum_fusion.2, s32[1024]{0:T(1024)S(1)} %broadcast_clamp_fusion), kind=kCustom, calls=%fused_computation | custom fusion | bytes 3149824 | tf_op jit(solution)/shard_map/gather | solution.py:129
  293.0 11.4 %all-to-all-done.3 = bf16[8,128,768]{2,1,0:T(8,128)(2,1)} async-done(((bf16[8,128,768]{2,1,0:T(8,128)(2,1)}), bf16[8,128,768]{2,1,0:T(8,128)(2,1)}, u32[]{:S(2)}, u32[]{:S(2)}) %all-to-all-start.3) | async-done | bytes 1572896 | tf_op jit(solution)/shard_map/all_to_all | solution.py:147
  307.3 7.4 %gather_fusion.1 = bf16[1024,768]{1,0:T(8,128)(2,1)} fusion(bf16[1280,768]{1,0:T(8,128)(2,1)} %pad_maximum_fusion.3, s32[1024]{0:T(1024)S(1)} %broadcast_clamp_fusion), kind=kCustom, calls=%fused_computation.1 | custom fusion | bytes 3149824 | tf_op jit(solution)/shard_map/gather | solution.py:176
  319.6 4.9 reshape.385
  324.5 6.8 %reduce_sum.185 = f32[512,768]{1,0:T(8,128)} reduce(f32[512,2,768]{2,1,0:T(2,128)} %reshape.386, f32[]{:T(128)} %constant.18.clone.1), dimensions={1}, to_apply=%region_14.15 | reduce | flops 393216 | bytes 4718596 | tf_op jit(solution)/shard_map/reduce_sum | solution.py:175
  334.5 16.3 %multiply_reduce_fusion.1 = f32[512,768]{1,0:T(8,128)S(1)} fusion(f32[512,2,768]{2,1,0:T(2,128)S(1)} %copy-done.6, f32[512,2]{1,0:T(8,128)} %copy.66), kind=kLoop, calls=%fused_computation.46 | loop fusion | flops 1179648 | bytes 4722688 | tf_op jit(solution)/shard_map/reduce_sum | solution.py:130
  362.0 11.0 %multiply_reduce_fusion = (f32[12,512]{1,0:T(8,128)S(1)}, f32[12,512,512]{1,2,0:T(8,128)}) fusion(f32[12,512]{1,0:T(8,128)S(1)} %copy-done.25, f32[12,512,512]{1,2,0:T(8,128)} %copy-done.1, pred[512,512]{0,1:T(8,128)(4,1)S(1)} %copy-done.15, bf16[512,12,64]{0,2,1:T(8,128)(2,1)S(1)} %bitcast.100, bf16[512,12,64]{0,2,1:T(8,128)(2,1)S(1)} %bitcast.99), kind=kOutput, calls=%fused_computation.15 | convolution fusion | flops 418375680 | bytes 27049984 | tf_op jit(solution)/shard_map/qhd,khd->hqk/dot_general | solution.py:195
  374.5 7.0 %multiply_convert_fusion = bf16[12,512,512]{1,2,0:T(8,128)(2,1)S(1)} fusion(f32[12,512,512]{1,2,0:T(8,128)} %get-tuple-element.60, f32[12,512]{1,0:T(8,128)S(1)} %get-tuple-element.59, f32[12,512]{1,0:T(8,128)S(1)} %copy-done.25, f32[12,512,512]{1,2,0:T(8,128)S(1)} %bitcast.91, pred[512,512]{0,1:T(8,128)(4,1)S(1)} %copy-done.15), kind=kLoop, calls=%fused_computation.14 | loop fusion | flops 18874368 | bytes 31768576 | tf_op jit(solution)/shard_map/convert_element_type | solution.py:199
  390.0 5.3 fusion.70
  402.2 40.2 %all-reduce = (f32[768]{0:T(1024)}, f32[768]{0:T(1024)}, f32[10]{0:T(128)}) all-reduce(f32[768]{0:T(1024)} %get-tuple-element.38, f32[768]{0:T(1024)} %get-tuple-element.36, f32[10]{0:T(128)} %convert_element_type.136), channel_id=1, replica_groups=mesh['dp'=4,'expert'=8] {'dp','expert'}, use_global_device_ids=true, to_apply=%region_21.22 | all-reduce | flops 1546 | bytes 12368 | tf_op jit(solution)/shard_map/psum | solution.py:228
  447.0 5.0 slice_bitcast_fusion
  458.1 128.8 %all-reduce.4.cloned.1.call-done = (f32[768,2304]{1,0:T(8,128)}, f32[768,768]{1,0:T(8,128)}) async-done(((f32[768,2304]{1,0:T(8,128)}, f32[768,768]{1,0:T(8,128)}), (f32[768,2304]{1,0:T(8,128)}, f32[768,768]{1,0:T(8,128)})) %all-reduce.4.cloned.1.call-update) | async-done | bytes 9437200 | tf_op jit(solution)/shard_map/psum | solution.py:228
  586.9 6.6 %copy.81 = f32[768,2304]{1,0:T(8,128)} copy(f32[768,2304]{1,0:T(8,128)} %get-tuple-element.66) | data formatting | bytes 14155776
  (202 shorter events, 136.4 us)
Async XLA Ops:
  7.2 20.0 %copy-start = (bf16[768,2304]{1,0:T(8,128)(2,1)S(1)}, bf16[768,2304]{1,0:T(8,128)(2,1)}, u32[]{:S(2)}) copy-start(bf16[768,2304]{1,0:T(8,128)(2,1)} %param.21) | copy-start | bytes 10616836
  7.2 123.7 %all-gather.3.cloned.1.call-start = ((), (), s32[]{:S(2)}) async-start(), calls=%async_computation.5 | async-start | bytes 5898240 | tf_op jit(solution)/shard_map/all_gather | solution.py:70
  9.6 22.3 %copy-start.31 = (f32[512]{0:T(512)}, f32[512]{0:T(512)S(1)}, u32[]{:S(2)}) copy-start(f32[512]{0:T(512)S(1)} %broadcast_multiply_fusion.2) | copy-start | bytes 6148
  11.1 12.5 %copy-start.37 = (f32[512]{0:T(512)}, f32[512]{0:T(512)S(1)}, u32[]{:S(2)}) copy-start(f32[512]{0:T(512)S(1)} %fusion.45) | copy-start | bytes 6148
  11.1 20.7 %copy-start.35 = (f32[512]{0:T(512)}, f32[512]{0:T(512)S(1)}, u32[]{:S(2)}) copy-start(f32[512]{0:T(512)S(1)} %fusion.77) | copy-start | bytes 6148
  40.3 7.0 %copy-start.45 = (s32[512]{0:T(512)S(1)}, s32[512]{0:T(512)}, u32[]{:S(2)}) copy-start(s32[512]{0:T(512)} %param.19) | copy-start | bytes 6148
  79.4 10.7 %copy-start.44 = (f32[512,2]{0,1:T(2,128)S(1)}, f32[512,2]{0,1:T(2,128)}, u32[]{:S(2)}) copy-start(f32[512,2]{0,1:T(2,128)} %param.17) | copy-start | bytes 12292
  82.1 44.5 %all-to-all-start = ((bf16[8,128,768]{2,1,0:T(8,128)(2,1)}), bf16[8,128,768]{2,1,0:T(8,128)(2,1)}, u32[]{:S(2)}, u32[]{:S(2)}) async-start(bf16[8,128,768]{2,1,0:T(8,128)(2,1)} %bitcast.96), calls=%async_computation | async-start | bytes 3145728 | tf_op jit(solution)/shard_map/all_to_all | solution.py:119
  89.4 89.4 %all-gather.5.cloned.1.call-start = ((), (), s32[]{:S(2)}) async-start(), calls=%async_computation.6 | async-start | bytes 5898240 | tf_op jit(solution)/shard_map/all_gather | solution.py:71
  126.5 40.9 %all-to-all-start.2 = ((bf16[8,128,768]{2,1,0:T(8,128)(2,1)}), bf16[8,128,768]{2,1,0:T(8,128)(2,1)}, u32[]{:S(2)}, u32[]{:S(2)}) async-start(bf16[8,128,768]{2,1,0:T(8,128)(2,1)} %bitcast.97), calls=%async_computation.2 | async-start | bytes 3145728 | tf_op jit(solution)/shard_map/all_to_all | solution.py:138
  130.8 316.2 %reduce-scatter.2.cloned.1.call-start = ((), (), s32[]{:S(2)}) async-start(), calls=%async_computation.7 | async-start | bytes 23592960 | tf_op jit(solution)/shard_map/reduce_scatter | solution.py:167
  194.4 8.3 %copy-start.49 = (bf16[1024,3072]{1,0:T(8,128)(2,1)}, bf16[1024,3072]{1,0:T(8,128)(2,1)S(1)}, u32[]{:S(2)}) copy-start(bf16[1024,3072]{1,0:T(8,128)(2,1)S(1)} %fusion.6) | copy-start | bytes 18874372
  194.4 8.3 %copy-start.11 = (f32[3072,768]{0,1:T(8,128)S(1)}, f32[3072,768]{0,1:T(8,128)}, u32[]{:S(2)}) copy-start(f32[3072,768]{0,1:T(8,128)} %fusion.98) | copy-start | bytes 28311556
  222.1 41.3 %all-to-all-start.1 = ((bf16[8,128,768]{2,1,0:T(8,128)(2,1)}), bf16[8,128,768]{2,1,0:T(8,128)(2,1)}, u32[]{:S(2)}, u32[]{:S(2)}) async-start(bf16[8,128,768]{2,1,0:T(8,128)(2,1)} %bitcast.106), calls=%async_computation.1 | async-start | bytes 3145728 | tf_op jit(solution)/shard_map/all_to_all | solution.py:125
  229.8 16.4 %slice-start.3 = ((s8[4718592]{0:T(1024)(128)(4,1)}), s8[524288]{0:T(1024)(128)(4,1)S(1)}, s32[]{:S(2)}) async-start(s8[4718592]{0:T(1024)(128)(4,1)} %bitcast.122), calls=%async_computation.12 | async-start | bytes 1048576
  229.8 16.4 %slice-start.5 = ((s8[6291456]{0:T(1024)(128)(4,1)}), s8[4194304]{0:T(1024)(128)(4,1)S(1)}, s32[]{:S(2)}) async-start(s8[6291456]{0:T(1024)(128)(4,1)} %bitcast.127), calls=%async_computation.14 | async-start | bytes 8388608
  238.6 7.5 %copy-start.19 = (f32[2,128,3072]{2,1,0:T(8,128)}, f32[2,128,3072]{2,1,0:T(8,128)S(1)}, u32[]{:S(2)}) copy-start(f32[2,128,3072]{2,1,0:T(8,128)S(1)} %fusion.104) | copy-start | bytes 9437188
  238.6 7.5 %slice-start.4 = ((s8[4718592]{0:T(1024)(128)(4,1)}), s8[4194304]{0:T(1024)(128)(4,1)S(1)}, s32[]{:S(2)}) async-start(s8[4718592]{0:T(1024)(128)(4,1)} %bitcast.122), calls=%async_computation.13 | async-start | bytes 8388608
  238.7 7.5 %slice-start.6 = ((s8[6291456]{0:T(1024)(128)(4,1)}), s8[2097152]{0:T(1024)(128)(4,1)S(1)}, s32[]{:S(2)}) async-start(s8[6291456]{0:T(1024)(128)(4,1)} %bitcast.127), calls=%async_computation.15 | async-start | bytes 4194304
  263.5 40.9 %all-to-all-start.3 = ((bf16[8,128,768]{2,1,0:T(8,128)(2,1)}), bf16[8,128,768]{2,1,0:T(8,128)(2,1)}, u32[]{:S(2)}, u32[]{:S(2)}) async-start(bf16[8,128,768]{2,1,0:T(8,128)(2,1)} %bitcast.105), calls=%async_computation.3 | async-start | bytes 3145728 | tf_op jit(solution)/shard_map/all_to_all | solution.py:147
  267.8 319.1 %all-reduce.4.cloned.1.call-start = ((), (), s32[]{:S(2)}) async-start(), calls=%async_computation.8 | async-start | bytes 18874368 | tf_op jit(solution)/shard_map/psum | solution.py:228
  324.4 6.8 %copy-start.28 = (f32[512]{0:T(512)S(1)}, f32[512]{0:T(512)}, u32[]{:S(2)}) copy-start(f32[512]{0:T(512)} %copy-done.27) | copy-start | bytes 6148
  324.4 6.8 %copy-start.30 = (f32[768]{0:T(1024)S(1)}, f32[768]{0:T(1024)}, u32[]{:S(2)}) copy-start(f32[768]{0:T(1024)} %param.23) | copy-start | bytes 9220
  324.4 6.8 %copy-start.34 = (f32[512]{0:T(512)S(1)}, f32[512]{0:T(512)}, u32[]{:S(2)}) copy-start(f32[512]{0:T(512)} %copy-done.33) | copy-start | bytes 6148
  324.4 10.0 %copy-start.40 = (f32[512]{0:T(512)S(1)}, f32[512]{0:T(512)}, u32[]{:S(2)}) copy-start(f32[512]{0:T(512)} %copy-done.39) | copy-start | bytes 6148
  334.4 16.4 %copy-start.3 = (f32[512,768]{1,0:T(8,128)S(1)}, f32[512,768]{1,0:T(8,128)}, u32[]{:S(2)}) copy-start(f32[512,768]{1,0:T(8,128)} %copy-done.2) | copy-start | bytes 4718596
  334.5 16.4 %copy-start.4 = (f32[512,768]{1,0:T(8,128)S(1)}, f32[512,768]{1,0:T(8,128)}, u32[]{:S(2)}) copy-start(f32[512,768]{1,0:T(8,128)} %reduce_sum.185) | copy-start | bytes 4718596
  361.9 11.1 %slice-start = ((s8[12582912]{0:T(1024)(128)(4,1)}), s8[4194304]{0:T(1024)(128)(4,1)S(1)}, s32[]{:S(2)}) async-start(s8[12582912]{0:T(1024)(128)(4,1)} %bitcast.90), calls=%async_computation.9 | async-start | bytes 8388608
  361.9 11.1 %slice-start.1 = ((s8[12582912]{0:T(1024)(128)(4,1)}), s8[4194304]{0:T(1024)(128)(4,1)S(1)}, s32[]{:S(2)}) async-start(s8[12582912]{0:T(1024)(128)(4,1)} %bitcast.90), calls=%async_computation.10 | async-start | bytes 8388608
  361.9 12.6 %slice-start.2 = ((s8[12582912]{0:T(1024)(128)(4,1)}), s8[4194304]{0:T(1024)(128)(4,1)S(1)}, s32[]{:S(2)}) async-start(s8[12582912]{0:T(1024)(128)(4,1)} %bitcast.90), calls=%async_computation.11 | async-start | bytes 8388608
  374.5 7.1 %copy-start.12 = (bf16[512,768]{0,1:T(8,128)(2,1)S(1)}, bf16[512,768]{0,1:T(8,128)(2,1)}, u32[]{:S(2)}) copy-start(bf16[512,768]{0,1:T(8,128)(2,1)} %copy.58) | copy-start | bytes 2359300
  586.9 6.6 %copy-start.21 = (f32[768,768]{1,0:T(8,128)S(1)}, f32[768,768]{1,0:T(8,128)}, u32[]{:S(2)}) copy-start(f32[768,768]{1,0:T(8,128)} %get-tuple-element.67) | copy-start | bytes 7077892
  (33 other events, 112.2 us)
Sparse Core Ops, SparseCore 0:
  9.6 40.1 all-gather.2
  91.8 38.8 all-gather.4
  209.7 138.4 reduce-scatter.1
  395.5 191.4 all-reduce.3
where the time goes:
time: 612 us; the launch traced here: 602 us
  waiting for transfers between devices  194 us (32%)
  matrix products  142 us (23%)
  local copies, waits for them, and re-layouts  107 us (17%)
  other arithmetic  83.4 us (14%)
  blocking collectives  40.2 us (7%)
  starting transfers between devices  20.8 us (3%)
  between operations  14.9 us (2%)
    psum x1, waiting for transfers between devices, body(): lax.psum((gain1_grad, w_qkv_grad, w_o_grad, gain2_grad, local_counts), ('...  129 us
    psum x1, blocking collectives, body(): lax.psum((gain1_grad, w_qkv_grad, w_o_grad, gain2_grad, local_counts), ('...  40.2 us
    all_to_all x1, waiting for transfers between devices, body(): lax.all_to_all(routed_grad, 'expert', split_axis=0, concat_axis=0, tiled=...  26.3 us
    unnamed x122, local copies, waits for them, and re-layouts  23.9 us
    dot_general x2, matrix products, expert_forward(): jnp.einsum('gcf,gfd->gcd', active, down_weights, preferred_element_type=j...  20 us
    dot_general x2, matrix products, expert_backward(): jnp.einsum('gcf,gfd->gcd', hidden_grad, up_weights, preferred_element_typ...  19.5 us
    dot_general x2, matrix products, expert_forward(): jnp.einsum('gcd,gfd->gcf', rows_low, up_weights, preferred_element_type=j...  19 us
    reduce_sum x1, other arithmetic, body(): output = mixed_rows + jnp.sum(picked * gates[:, :, None], axis=1)  16.3 us
  transfers between devices with their start and end apart: 8, of which 5 were waited for; matrix products, arithmetic and copies ran while one was open for 48% of the time, Pallas kernels for 0%

commit v1 on v0

v1 whole, which is shorter than its diff:
```python
import functools
import jax
import jax.numpy as jnp
from jax import lax
from jax.experimental import pallas as pl
from jax.experimental.pallas import tpu as pltpu
from jax.sharding import PartitionSpec as P

MESH = pl.DeviceIdType.MESH


def butterfly(dp_size, ex_size):
    core = ("dp", 1)
    xs = [("dp", 2 << k) for k in range((dp_size // 2).bit_length() - 1)]
    depth = 4 if ex_size % 4 == 0 else 1
    wide = ex_size // depth
    ys = [("expert", 1 << k) for k in range(wide.bit_length() - 1)]
    zs = [("expert", wide << k) for k in range(depth.bit_length() - 1)]
    return core, xs, ys, zs


def group_of(stage):
    place = {"dp": lax.axis_index("dp"), "expert": lax.axis_index("expert")}
    mine = sum(lax.rem(place[axis] // mask, 2) << j for j, (axis, mask) in enumerate(stage))
    peers = []
    for m in range(1, 1 << len(stage)):
        peer = dict(place)
        for j, (axis, mask) in enumerate(stage):
            if m >> j & 1:
                peer[axis] = peer[axis] ^ mask
        peers.append((peer["dp"], peer["expert"]))
    return mine, peers


def dot_nn(a, b):
    return jnp.dot(a, b, preferred_element_type=jnp.float32)


def dot_nt(a, b):
    return lax.dot_general(a, b, (((1,), (1,)), ((), ())), preferred_element_type=jnp.float32)


def dot_tn(a, b):
    return lax.dot_general(a, b, (((0,), (0,)), ((), ())), preferred_element_type=jnp.float32)


GELU_A = 0.7978845608028654
GELU_B = GELU_A * 0.044715


def gelu_pair(h):
    square = h * h
    bend = jnp.tanh(h * (GELU_B * square + GELU_A))
    share = 0.5 * bend + 0.5
    slope = share + (0.5 * h) * (1.0 - bend * bend) * ((3.0 * GELU_B) * square + GELU_A)
    return h * share, slope


def remote(source, target, pair, at, device):
    return pltpu.make_async_remote_copy(
        src_ref=source, dst_ref=target, send_sem=pair.at[(0,) + at], recv_sem=pair.at[(1,) + at], device_id=device,
        device_id_type=MESH)


class Gather:

    def __init__(self, dp, ex, far, source, whole, sems):
        self.dp, self.ex, self.far, self.source, self.whole, self.sems = dp, ex, far, source, whole, sems
        self.rows = source.shape[0]

    def at(self, which):
        return self.whole.at[pl.ds(pl.multiple_of(which * self.rows, 16), self.rows)]

    def first(self, k):
        return remote(self.source, self.at(self.dp), self.sems, (0, k), (self.dp ^ (2 * k if k else 1), self.ex))

    def second(self, k):
        theirs = self.at(self.dp ^ (2 * k))
        return remote(theirs, theirs, self.sems, (1, k), (self.dp ^ 1, self.ex))

    def start(self):
        for k in list(range(1, self.far)) + [0]:
            self.first(k).start()

    def forward(self):
        for k in range(1, self.far):
            self.first(k).wait_recv()
            self.second(k).start()

    def finish(self):
        self.first(0).wait()
        for k in range(1, self.far):
            self.first(k).wait_send()
            self.second(k).wait()


class Scatter:

    def __init__(self, dp, ex, far, source, core_v, pre_v, chip_v, sems):
        self.dp, self.ex, self.far, self.source = dp, ex, far, source
        self.core_v, self.pre_v, self.chip_v, self.sems = core_v, pre_v, chip_v, sems
        self.rows = core_v.shape[1]

    def at(self, which):
        return self.source.at[pl.ds(pl.multiple_of(which * self.rows, 16), self.rows)]

    def core(self, k):
        return remote(self.at(self.dp ^ (2 * k + 1)), self.core_v.at[k], self.sems, (0, k), (self.dp ^ 1, self.ex))

    def chip(self, k):
        return remote(self.pre_v.at[k - 1], self.chip_v.at[k - 1], self.sems, (1, k), (self.dp ^ (2 * k), self.ex))

    def to_chips(self):
        for k in range(1, self.far):
            self.core(k).wait_recv()
            source = self.at(self.dp ^ (2 * k))

            def add(j, _):
                at = pl.ds(pl.multiple_of(j * 128, 128), 128)
                total = source[at, :].astype(jnp.float32) + self.core_v[k, at, :].astype(jnp.float32)
                self.pre_v[k - 1, at, :] = total.astype(jnp.bfloat16)
                return 0

            lax.fori_loop(0, self.rows // 128, add, 0)
            self.chip(k).start()

    def finish(self):
        self.core(0).wait_recv()
        for k in range(1, self.far):
            self.chip(k).wait_recv()
        source = self.at(self.dp)

        def add(j, _):
            at = pl.ds(pl.multiple_of(j * 128, 128), 128)
            total = source[at, :].astype(jnp.float32) + self.core_v[0, at, :].astype(jnp.float32)
            for k in range(1, self.far):
                total = total + self.chip_v[k - 1, at, :].astype(jnp.float32)
            self.core_v[0, at, :] = total.astype(jnp.bfloat16)
            return 0

        lax.fori_loop(0, self.rows // 128, add, 0)
        for k in range(self.far):
            self.core(k).wait_send()
            if k:
                self.chip(k).wait_send()


class Sums:

    def __init__(self, chunks, blocks, acc, got, out, scatter_sems, gather_sems, own_sems):
        self.chunks, self.blocks, self.acc, self.got, self.out = chunks, blocks, acc, got, out
        self.scatter_sems, self.gather_sems, self.own_sems = scatter_sems, gather_sems, own_sems
        self.offs = [[base] for base, _, _, _ in chunks]
        self.lens = [[rows] for _, rows, _, _ in chunks]
        self.land = [[base] for base, _, _, _ in chunks]
        self.copies = [None] * len(chunks)
        self.shift = [0] * len(chunks)
        self.stage = [0] * len(chunks)
        self.own = [None] * len(chunks)

    def scatter(self, c, i):
        base, _, order, _ = self.chunks[c]
        mine, peers = group_of(order[i])
        part = self.lens[c][i] >> len(order[i])
        source = self.acc if i else self.blocks
        self.copies[c] = []
        for m, peer in enumerate(peers, 1):
            give = pl.multiple_of(self.offs[c][i] + (mine ^ m) * part + self.shift[c], 16)
            self.copies[c].append(remote(
                source.at[pl.ds(give, part)], self.got.at[pl.ds(self.land[c][i] + (m - 1) * part, part)],
                self.scatter_sems, (c, i, m), peer))
            self.copies[c][-1].start()
        self.offs[c].append(self.offs[c][i] + mine * part)
        self.lens[c].append(part)
        self.land[c].append(self.land[c][i] + len(peers) * part)

    def gather(self, c, i):
        stages = len(self.chunks[c][2])
        _, peers = group_of(self.chunks[c][2][i])
        part = self.lens[c][i + 1]
        target = self.out.at[pl.ds(pl.multiple_of(self.offs[c][i + 1], 16), part)]
        source = target
        if i + 1 == stages:
            source = self.acc.at[pl.ds(pl.multiple_of(self.offs[c][i + 1] + self.shift[c], 16), part)]
            self.own[c] = pltpu.make_async_copy(source, target, self.own_sems.at[c])
            self.own[c].start()
        self.copies[c] = []
        for m, peer in enumerate(peers, 1):
            self.copies[c].append(remote(source, target, self.gather_sems, (c, i, m), peer))
            self.copies[c][-1].start()

    def start(self, phase):
        for c, chunk in enumerate(self.chunks):
            if chunk[3] == phase:
                self.scatter(c, 0)

    def advance(self, c):
        if not self.copies[c]:
            return
        base, _, order, _ = self.chunks[c]
        stages, s = len(order), self.stage[c]
        for copy in self.copies[c]:
            copy.wait()
        self.stage[c] += 1
        if s >= stages:
            i = 2 * stages - 1 - s
            self.copies[c] = None
            if s == stages:
                self.own[c].wait()
            if i > 0:
                self.gather(c, i - 1)
            return
        part = self.lens[c][s + 1]
        source = self.acc if s else self.blocks
        keep, begin = self.offs[c][s + 1], self.land[c][s]
        count = (1 << len(order[s])) - 1
        tile = part
        while tile > 128 or part % tile or tile % 16:
            tile -= 16
        move_in = self.shift[c]
        if s == 0:
            self.shift[c] = base // 2 - keep
        move_out = self.shift[c]

        def add(j, _):
            at = pl.ds(pl.multiple_of(keep + move_out + j * tile, 16), tile)
            come = pl.ds(pl.multiple_of(keep + move_in + j * tile, 16), tile)
            total = source[come, :].astype(jnp.float32)
            for m in range(count):
                other = pl.ds(pl.multiple_of(begin + m * part + j * tile, 16), tile)
                total = total + self.got[other, :].astype(jnp.float32)
            self.acc[at, :] = total.astype(jnp.bfloat16)
            return 0

        lax.fori_loop(0, part // tile, add, 0)
        if s + 1 < stages:
            self.scatter(c, s + 1)
        else:
            self.gather(c, s)

    def tick(self):
        for c in reversed(range(len(self.chunks))):
            self.advance(c)

    def finish(self):
        while any(self.copies):
            self.tick()


def sum_chunks(dp_size, ex_size, rows):
    core, xs, ys, zs = butterfly(dp_size, ex_size)
    yxz, xyz, zyx = [[core], ys, xs, zs], [[core], xs, ys, zs], [[core], zs, ys, xs]
    if dp_size * ex_size * 16 <= 512:
        return [(0, 1536, yxz, 0), (1536, 2048, yxz, 1), (3584, 1024, yxz, 2), (4608, 1024, xyz, 2), (5632, 512, zyx, 2)]
    third = rows // 3
    return [(0, third, yxz, 2), (third, third, xyz, 2), (2 * third, third, zyx, 2)]


def layer_kernel(dp_size, ex_size, kinds, cap,
                 lengths_s, chosen_ref, gatest_ref, keep_ref, gates_ref, tok_ref, cot_ref, gain1_ref, gain2_ref,
                 wqkv_hbm, wo_hbm, in_hbm, outw_hbm, fin_hbm, fout_hbm,
                 out_ref, dtok_ref, total_hbm, sum_ref, dwin_hbm, dwout_hbm,
                 back_hbm, ret_hbm, proj_hbm, prob_hbm, attt_hbm, normt_hbm,
                 token_st, grad_st, rows_v, grad_v, win_v, wout_v, icore_v, ipre_v, ichip_v, ocore_v, opre_v, ochip_v,
                 got_v, mixed_v, place_v, column_v, gain_v, count_v, small_v,
                 grad_sem, row_sem, back_sem, res_sem, win_sem, wout_sem, iscat_sem, oscat_sem, part_sem, join_sem, own_sem,
                 tiny_sem, local_sem, prob_sem):
    dp = lax.axis_index("dp")
    ex = lax.axis_index("expert")
    count, feat = tok_ref.shape
    shard = in_hbm.shape[0]
    hidden = win_v.shape[0]
    far = dp_size // 2
    slots = kinds * cap
    padded = token_st.shape[0]
    full, low = jnp.float32, jnp.bfloat16
    dma = pltpu.SemaphoreType.DMA
    half, wide, pairs, tiles = count // 2, feat // 2, feat // 128, hidden // 256

    barrier = pltpu.get_barrier_semaphore()
    for r in range(1, ex_size):
        pl.semaphore_signal(barrier, inc=1, device_id=(dp, ex ^ r), device_id_type=MESH)
    for k in range(1, dp_size):
        pl.semaphore_signal(barrier, inc=1, device_id=(dp ^ k, ex), device_id_type=MESH)

    def slot_rows(which):
        return pl.ds(pl.multiple_of(which * cap, 16), cap)

    def grad_copy(r):
        return remote(grad_st.at[slot_rows(2 + (ex ^ r))], grad_v.at[pl.ds(r * cap, cap)], grad_sem, (r,), (dp, ex ^ r))

    def row_copy(r):
        return remote(token_st.at[slot_rows(2 + (ex ^ r))], rows_v.at[pl.ds(r * cap, cap)], row_sem, (r,), (dp, ex ^ r))

    def result_copy(r):
        source, target = rows_v.at[pl.ds(r * cap, cap)], ret_hbm.at[slot_rows(2 + ex)]
        if r == 0:
            return pltpu.make_async_copy(source, target, local_sem.at[0])
        return remote(source, target, res_sem, (r,), (dp, ex ^ r))

    win = Gather(dp, ex, far, in_hbm, win_v, win_sem)
    wout = Gather(dp, ex, far, outw_hbm, wout_v, wout_sem)
    in_scatter = Scatter(dp, ex, far, win_v, icore_v, ipre_v, ichip_v, iscat_sem)
    out_scatter = Scatter(dp, ex, far, wout_v, ocore_v, opre_v, ochip_v, oscat_sem)

    def own_shards():
        return [pltpu.make_async_copy(outw_hbm, wout.at(dp), local_sem.at[1]),
                pltpu.make_async_copy(in_hbm, win.at(dp), local_sem.at[2])]

    def forward(wqkv_v, wo_v, norm_v, normt_v, proj_v, prob_v, attt_v, att_v, bias_v, sem):
        loads = [pltpu.make_async_copy(wqkv_hbm, wqkv_v, sem.at[0]), pltpu.make_async_copy(wo_hbm, wo_v, sem.at[1])]
        for copy in loads + own_shards():
            copy.start()

        kind = lax.broadcasted_iota(jnp.int32, (128, count), 0)
        first = chosen_ref[0:1, :]
        second = chosen_ref[1:2, :]
        hit_first = jnp.where(kind == first, 1.0, 0.0)
        hit_second = jnp.where(kind == second, 1.0, 0.0)
        hits = (hit_first + hit_second).astype(low)
        before = jnp.where(lax.broadcasted_iota(jnp.int32, (count, count), 0)
                           < lax.broadcasted_iota(jnp.int32, (count, count), 1), 1.0, 0.0).astype(low)
        ahead = dot_nn(hits, before)
        count_v[...] = dot_nt(jnp.ones((8, count), low), hits)
        place_v[0:1, :] = first.astype(full) * cap + jnp.sum(hit_first * ahead, axis=0, keepdims=True)
        place_v[1:2, :] = second.astype(full) * cap + jnp.sum(hit_second * ahead, axis=0, keepdims=True)

        def picks(which):
            slot = (which * cap + lax.broadcasted_iota(jnp.int32, (cap, count), 0)).astype(full)
            return slot == place_v[0:1, :], slot == place_v[1:2, :]

        def grad_rows(which):
            one, two = picks(which)
            gate = jnp.sum(jnp.where(one, gatest_ref[0:1, :], jnp.where(two, gatest_ref[1:2, :], 0.0)), axis=1,
                           keepdims=True)
            pick = jnp.where(one | two, 1.0, 0.0).astype(low)
            return (dot_nn(pick, cot_ref[...]) * gate).astype(low)

        pl.semaphore_wait(barrier, ex_size - 1 + dp_size - 1)
        wout.start()
        for r in reversed(range(ex_size)):
            if r:
                grad_st[slot_rows(2 + (ex ^ r)), :] = grad_rows(2 + (ex ^ r))
                grad_copy(r).start()
            else:
                grad_v[0:cap, :] = grad_rows(2 + ex)
        for which in range(2):
            grad_st[slot_rows(which), :] = grad_rows(which)
        if padded > slots:
            grad_st[slots:, :] = jnp.zeros((padded - slots, feat), low)
            token_st[slots:, :] = jnp.zeros((padded - slots, feat), low)

        spot = lax.broadcasted_iota(jnp.int32, (1, count), 1)
        document = jnp.zeros((1, count), full)
        end = lengths_s[0, 0]
        for j in range(1, lengths_s.shape[1] + 1):
            document = document + jnp.where(spot >= end, 1.0, 0.0)
            if j < lengths_s.shape[1]:
                end = end + lengths_s[0, j]
        place_v[2:3, :] = document
        place_v[3:4, :] = keep_ref[...].astype(full)
        place_v[4:8, :] = jnp.zeros((4, count), full)
        columns = place_v[...].T
        column_v[...] = columns

        def norm_rows(i, source, gain, target):
            at = pl.ds(pl.multiple_of(i * 64, 64), 64)
            whole = source[at, :].astype(full)
            centred = whole - jnp.mean(whole, axis=1, keepdims=True)
            scale = lax.rsqrt(jnp.mean(centred * centred, axis=1, keepdims=True) + 1e-05)
            target[at, :] = (centred * scale * gain).astype(low)
            return 0

        lax.fori_loop(0, count // 64, lambda i, _: norm_rows(i, tok_ref, gain1_ref[...][None], norm_v), 0)
        loads[0].wait()

        def project(n, _):
            at = pl.ds(pl.multiple_of(n * 256, 256), 256)
            proj_v[:, at] = dot_nn(norm_v[...], wqkv_v[:, at]).astype(low)
            return 0

        lax.fori_loop(0, 3 * feat // 256, project, 0)
        stores = [pltpu.make_async_copy(proj_v, proj_hbm, sem.at[2])]
        stores[-1].start()

        key = lax.broadcasted_iota(jnp.int32, (count, count), 0)
        query = lax.broadcasted_iota(jnp.int32, (count, count), 1)
        allowed = (columns[:, 2:3] == document) & (key <= query) & ((columns[:, 3:4] > 0.0) | (key == query))
        bias_v[...] = jnp.where(allowed, 0.0, -1e30)
        lower = lax.broadcasted_iota(jnp.int32, (count, 128), 1) < 64

        def head_pair(p, _):
            at = pl.multiple_of(p * 128, 128)
            q = proj_v[:, pl.ds(at, 128)]
            k = proj_v[:, pl.ds(pl.multiple_of(feat + p * 128, 128), 128)]
            vt = proj_v[:, pl.ds(pl.multiple_of(2 * feat + p * 128, 128), 128)].T
            for j in range(2):
                one = jnp.where(lower if j == 0 else jnp.logical_not(lower), k, jnp.zeros_like(k))
                for b in range(2):
                    reach, here = (b + 1) * half, slice(b * half, (b + 1) * half)
                    scores = dot_nt(one[0:reach], q[here]) * 0.125 + bias_v[0:reach, here]
                    powers = jnp.exp(scores - jnp.max(scores, axis=0, keepdims=True))
                    probs = (powers * (1.0 / jnp.sum(powers, axis=0, keepdims=True))).astype(low)
                    prob_v[2 * p + j, b * half:b * half + reach, :] = probs
                    attt_v[pl.ds(at + 64 * j, 64), here] = dot_nn(vt[64 * j:64 * j + 64, 0:reach], probs).astype(low)
            pltpu.make_async_copy(prob_v.at[pl.ds(2 * p, 2)], prob_hbm.at[pl.ds(2 * p, 2)], prob_sem.at[p]).start()
            return 0

        lax.fori_loop(0, pairs, head_pair, 0)
        win.start()
        stores.append(pltpu.make_async_copy(attt_v, attt_hbm, sem.at[3]))
        stores[-1].start()

        def turn(n, _):
            at = pl.ds(pl.multiple_of(n * 128, 128), 128)
            att_v[:, at] = attt_v[at, :].T
            return 0

        lax.fori_loop(0, pairs, turn, 0)
        loads[1].wait()

        def mix(n, _):
            at = pl.ds(pl.multiple_of(n * 256, 256), 256)
            mixed_v[:, at] = tok_ref[:, at].astype(full) + dot_nn(att_v[...], wo_v[:, at])
            return 0

        lax.fori_loop(0, feat // 256, mix, 0)
        lax.fori_loop(0, count // 64, lambda i, _: norm_rows(i, mixed_v, gain2_ref[...][None], att_v), 0)

        def token_rows(which):
            one, two = picks(which)
            return dot_nn(jnp.where(one | two, 1.0, 0.0).astype(low), att_v[...]).astype(low)

        for r in reversed(range(ex_size)):
            if r:
                token_st[slot_rows(2 + (ex ^ r)), :] = token_rows(2 + (ex ^ r))
                row_copy(r).start()
            else:
                rows_v[0:cap, :] = token_rows(2 + ex)
        for which in range(2):
            token_st[slot_rows(which), :] = token_rows(which)

        def turn_norm(n, _):
            at = pl.ds(pl.multiple_of(n * 128, 128), 128)
            normt_v[at, :] = norm_v[:, at].T
            return 0

        lax.fori_loop(0, pairs, turn_norm, 0)
        stores.append(pltpu.make_async_copy(normt_v, normt_hbm, sem.at[4]))
        stores[-1].start()
        for p in range(pairs):
            pltpu.make_async_copy(prob_v.at[pl.ds(2 * p, 2)], prob_hbm.at[pl.ds(2 * p, 2)], prob_sem.at[p]).wait()
        for copy in stores:
            copy.wait()

    heads = feat // 64
    pl.run_scoped(
        forward, pltpu.VMEM((feat, 3 * feat), low), pltpu.VMEM((feat, feat), low), pltpu.VMEM((count, feat), low),
        pltpu.VMEM((feat, count), low), pltpu.VMEM((count, 3 * feat), low), pltpu.VMEM((heads, count + half, half), low),
        pltpu.VMEM((feat, count), low), pltpu.VMEM((count, feat), low), pltpu.VMEM((count, count), full), dma((5,)))

    def expert(act_v, hg_v, fin_v, fout_v, facc_v, fst_v, rg_v, sem, load_sem):
        steps = fin_hbm.shape[0]
        per = steps // 2

        def frozen_load(i, slot):
            return (pltpu.make_async_copy(fin_hbm.at[i], fin_v.at[slot], load_sem.at[0, slot]),
                    pltpu.make_async_copy(fout_hbm.at[i], fout_v.at[slot], load_sem.at[1, slot]))

        def back_copy(r):
            source, target = rg_v.at[pl.ds(r * cap, cap)], back_hbm.at[slot_rows(2 + ex)]
            if r == 0:
                return pltpu.make_async_copy(source, target, sem.at[0])
            return remote(source, target, back_sem, (r,), (dp, ex ^ r))

        for copy in frozen_load(0, 0):
            copy.start()

        def frozen(i, _):
            slot = lax.rem(i, 2)
            for copy in frozen_load(i, slot):
                copy.wait()

            @pl.when(i + 1 < steps)
            def _():
                for copy in frozen_load(i + 1, 1 - slot):
                    copy.start()
            which = i // per
            up, down = fin_v[slot], fout_v[slot]
            active, slope = gelu_pair(dot_nt(token_st[slot_rows(which), :], up))
            slope_in = dot_nt(grad_st[slot_rows(which), :], down)
            result = dot_nn(active.astype(low), down)
            back = dot_nn((slope_in * slope).astype(low), up)
            fresh = lax.rem(i, per) == 0

            @pl.when(fresh)
            def _():
                facc_v[0, which] = result
                facc_v[1, which] = back

            @pl.when(jnp.logical_not(fresh))
            def _():
                facc_v[0, which] += result
                facc_v[1, which] += back
            return 0

        lax.fori_loop(0, steps, frozen, 0)
        stores = []
        for which in range(2):
            fst_v[0, pl.ds(which * cap, cap), :] = facc_v[0, which].astype(low)
            fst_v[1, pl.ds(which * cap, cap), :] = facc_v[1, which].astype(low)
        for n, target in enumerate((ret_hbm, back_hbm)):
            stores.append(pltpu.make_async_copy(fst_v.at[n], target.at[pl.ds(0, 2 * cap)], sem.at[1 + n]))
            stores[-1].start()
        wout.forward()
        for copy in own_shards():
            copy.wait()
        wout.finish()
        for r in range(1, ex_size):
            grad_copy(r).wait()

        def slope_tile(t, _):
            at = pl.ds(pl.multiple_of(t * 256, 256), 256)
            hg_v[:, at] = dot_nt(grad_v[...], wout_v[at, :]).astype(low)
            return 0

        lax.fori_loop(0, tiles, slope_tile, 0)
        win.forward()
        win.finish()
        order = list(reversed(range(ex_size)))
        for group in (order[:ex_size // 4], order[ex_size // 4:ex_size // 2], order[ex_size // 2:]):
            here = pl.ds(group[-1] * cap, len(group) * cap)
            for r in group:
                if r:
                    row_copy(r).wait_recv()

            def hidden_tile(t, _, here=here):
                at = pl.ds(pl.multiple_of(t * 256, 256), 256)
                active, slope = gelu_pair(dot_nt(rows_v[here, :], win_v[at, :]))
                act_v[here, at] = active.astype(low)
                hg_v[here, at] = (hg_v[here, at].astype(full) * slope).astype(low)
                return 0

            lax.fori_loop(0, tiles, hidden_tile, 0)

            def back_tile(n, _, here=here):
                at = pl.ds(pl.multiple_of(n * 256, 256), 256)
                rg_v[here, at] = dot_nn(hg_v[here, :], win_v[:, at]).astype(low)
                return 0

            lax.fori_loop(0, feat // 256, back_tile, 0)
            for r in group:
                back_copy(r).start()
        for r in range(1, ex_size):
            row_copy(r).wait_send()

        width = 256 if shard % 256 == 0 else 128

        def one_shard(which, units, rows, target):
            def tile(j, _):
                at = pl.ds(pl.multiple_of(which * shard + j * width, width), width)
                target[at, :] = dot_tn(units[:, at], rows[...]).astype(low)
                return 0

            lax.fori_loop(0, shard // width, tile, 0)

        def all_shards(scatter, units, rows):
            for k in range(1, far):
                one_shard(dp ^ (2 * k + 1), units, rows, scatter.source)
                scatter.core(k).start()
                one_shard(dp ^ (2 * k), units, rows, scatter.source)
            scatter.to_chips()
            one_shard(dp ^ 1, units, rows, scatter.source)
            scatter.core(0).start()
            one_shard(dp, units, rows, scatter.source)

        all_shards(in_scatter, hg_v, rows_v)

        def result_tile(n, _):
            at = pl.ds(pl.multiple_of(n * 256, 256), 256)
            rows_v[:, at] = dot_nn(act_v[...], wout_v[:, at]).astype(low)
            return 0

        lax.fori_loop(0, feat // 256, result_tile, 0)
        for r in reversed(range(ex_size)):
            result_copy(r).start()
        all_shards(out_scatter, act_v, grad_v)
        for copy in stores:
            copy.wait()
        for r in range(ex_size):
            back_copy(r).wait()

    span = fin_hbm.shape[1]
    rows_all = ex_size * cap
    pl.run_scoped(
        expert, pltpu.VMEM((rows_all, hidden), low), pltpu.VMEM((rows_all, hidden), low), pltpu.VMEM((2, span, feat), low),
        pltpu.VMEM((2, span, feat), low), pltpu.VMEM((2, 2, cap, feat), full), pltpu.VMEM((2, 2 * cap, feat), low),
        pltpu.VMEM((rows_all, feat), low), dma((3,)), dma((2, 2)))

    back_v, ret_v, branch_v, da_v = grad_st, token_st, grad_v.at[pl.ds(0, count)], grad_v.at[pl.ds(count, count)]

    def backward(prob_v, proj_v, turned_v, wo_v, pg_v, blocks_v, acc_v, g_v, mg_v, pick_v, dqt_v, sem):
        loads = [pltpu.make_async_copy(source, target, sem.at[i]) for i, (source, target) in enumerate([
            (back_hbm, back_v.at[pl.ds(0, slots)]), (attt_hbm, turned_v), (wo_hbm, wo_v), (prob_hbm, prob_v),
            (proj_hbm, proj_v)])]
        for copy in loads:
            copy.start()
        sums = Sums(sum_chunks(dp_size, ex_size, blocks_v.shape[0]), blocks_v, acc_v, got_v, total_hbm, part_sem, join_sem,
                    own_sem)

        def place_tile(n):
            at = pl.ds(pl.multiple_of(n * 128, 128), 128)
            slot = (n * 128 + lax.broadcasted_iota(jnp.int32, (count, 128), 1)).astype(full)
            return at, slot == column_v[:, 0:1], slot == column_v[:, 1:2]

        def pick_both(n, _):
            at, one, two = place_tile(n)
            pick_v[:, at] = jnp.where(one | two, 1.0, 0.0).astype(low)
            return 0

        lax.fori_loop(0, padded // 128, pick_both, 0)
        loads[0].wait()

        def collect(n, _):
            at = pl.ds(pl.multiple_of(n * 256, 256), 256)
            g_v[:, at] = dot_nn(pick_v[...], back_v[:, at])
            return 0

        lax.fori_loop(0, feat // 256, collect, 0)
        gain_v[...] = jnp.zeros_like(gain_v)
        gain_v[16:24, 0:128] = count_v[...]

        def norm_back(i, whole, gain, target):
            at = pl.ds(pl.multiple_of(i * 64, 64), 64)
            centred = whole - jnp.mean(whole, axis=1, keepdims=True)
            scale = lax.rsqrt(jnp.mean(centred * centred, axis=1, keepdims=True) + 1e-05)
            unit = centred * scale
            grad = g_v[at, :]
            weighted = grad * unit
            gain_v[target:target + 8, :] += jnp.sum(weighted.reshape(8, 8, feat), axis=0)
            scaled = grad * gain
            return at, scale * (scaled - jnp.mean(scaled, axis=1, keepdims=True)
                                - unit * jnp.mean(scaled * unit, axis=1, keepdims=True))

        def second_norm(i, _):
            at, part = norm_back(i, mixed_v[pl.ds(pl.multiple_of(i * 64, 64), 64), :], gain2_ref[...][None], 8)
            grad = cot_ref[at, :].astype(full) + part
            mg_v[at, :] = grad
            branch_v[at, :] = grad.astype(low)
            return 0

        lax.fori_loop(0, count // 64, second_norm, 0)
        loads[1].wait()

        def out_weight(b, _):
            at = pl.ds(pl.multiple_of(b * wide, 128), wide)
            blocks_v[pl.ds(pl.multiple_of(b * feat, 16), feat), :] = dot_nn(turned_v[...], branch_v[:, at]).astype(low)
            return 0

        lax.fori_loop(0, 2, out_weight, 0)
        loads.append(pltpu.make_async_copy(normt_hbm, turned_v, sem.at[5]))
        loads[5].start()
        sums.start(0)
        loads[2].wait()

        def attended_grad(n, _):
            at = pl.ds(pl.multiple_of(n * 256, 256), 256)
            da_v[:, at] = dot_nt(branch_v[...], wo_v[at, :]).astype(low)
            return 0

        lax.fori_loop(0, feat // 256, attended_grad, 0)
        loads[3].wait()
        loads[4].wait()
        lower = lax.broadcasted_iota(jnp.int32, (count, 128), 1) < 64

        def head_pair(p, _):
            at_q = pl.ds(pl.multiple_of(p * 128, 128), 128)
            at_k = pl.ds(pl.multiple_of(feat + p * 128, 128), 128)
            at_v = pl.ds(pl.multiple_of(2 * feat + p * 128, 128), 128)
            q, k, v, da = proj_v[:, at_q], proj_v[:, at_k], proj_v[:, at_v], da_v[:, at_q]
            kt = k.T
            key_near = key_far = value_near = value_far = 0.0
            for j in range(2):
                mask = lower if j == 0 else jnp.logical_not(lower)
                qj, vj, daj = [jnp.where(mask, w, jnp.zeros_like(w)) for w in (q, v, da)]
                for b in range(2):
                    reach, here = (b + 1) * half, slice(b * half, (b + 1) * half)
                    prob = prob_v[2 * p + j, b * half:b * half + reach, :]
                    whole = prob.astype(full)
                    grad = dot_nt(vj[0:reach], da[here])
                    score = (whole * (grad - jnp.sum(whole * grad, axis=0, keepdims=True))).astype(low)
                    dqt_v[64 * j:64 * j + 64, here] = dot_nn(kt[64 * j:64 * j + 64, 0:reach], score)
                    key_near += dot_nn(score[0:half], qj[here])
                    value_near += dot_nn(prob[0:half], daj[here])
                    if b:
                        key_far += dot_nn(score[half:], qj[here])
                        value_far += dot_nn(prob[half:], daj[here])
            pg_v[:, at_q] = (dqt_v[...].T * 0.125).astype(low)
            pg_v[0:half, at_k] = (key_near * 0.125).astype(low)
            pg_v[half:, at_k] = (key_far * 0.125).astype(low)
            pg_v[0:half, at_v] = value_near.astype(low)
            pg_v[half:, at_v] = value_far.astype(low)
            return 0

        for part in range(2):
            lax.fori_loop(part * pairs // 2, (part + 1) * pairs // 2, head_pair, 0)
            if part == 0:
                loads[5].wait()
                in_scatter.finish()
                ends = [pltpu.make_async_copy(icore_v.at[0], dwin_hbm, sem.at[7])]
                ends[-1].start()
                weights = [pltpu.make_async_copy(wqkv_hbm.at[:, pl.ds(c * feat, feat)], win_v.at[pl.ds(c * feat, feat)],
                                                 sem.at[10 + c]) for c in range(3)]
                for copy in weights:
                    copy.start()
            sums.tick()

            def weight_block(c, _, part=part):
                at = pl.ds(pl.multiple_of(c * feat + part * wide, 128), wide)
                into = pl.ds(pl.multiple_of(2 * feat + (3 * part + c) * feat, 16), feat)
                blocks_v[into, :] = dot_nn(turned_v[...], pg_v[:, at]).astype(low)
                return 0

            lax.fori_loop(0, 3, weight_block, 0)
            sums.start(1 + part)
        for copy in weights:
            copy.wait()

        def norm_grad(n, _):
            at = pl.ds(pl.multiple_of(n * 256, 256), 256)
            g_v[:, at] = sum(dot_nt(pg_v[:, c * feat:(c + 1) * feat],
                                    win_v[pl.ds(pl.multiple_of(c * feat + n * 256, 256), 256), :]) for c in range(3))
            return 0

        lax.fori_loop(0, feat // 256, norm_grad, 0)
        sums.tick()

        def first_norm(i, _):
            here = pl.ds(pl.multiple_of(i * 64, 64), 64)
            at, part = norm_back(i, tok_ref[here, :].astype(full), gain1_ref[...][None], 0)
            dtok_ref[at, :] = (mg_v[at, :] + part).astype(low)
            return 0

        lax.fori_loop(0, count // 64, first_norm, 0)

        order = sums.chunks[0][2]
        stages = len(order)
        slot_of = [stages + sum((1 << len(stage)) - 1 for stage in order[:i]) for i in range(stages)]
        for i in range(3):
            small_v[0, i:i + 1, :] = jnp.sum(gain_v[8 * i:8 * i + 8, :], axis=0, keepdims=True)
        small_v[0, 2:3, :] = gain_v[16:17, :]
        small_v[0, 3:8, :] = jnp.zeros((5, feat), full)

        def small_send(i):
            copies = []
            for m, peer in enumerate(group_of(order[i])[1], 1):
                copies.append(remote(small_v.at[i], small_v.at[slot_of[i] + m - 1], tiny_sem, (i, m), peer))
                copies[-1].start()
            return copies

        def small_add(i, copies):
            for copy in copies:
                copy.wait()
            mine, peers = group_of(order[i])
            total = jnp.zeros_like(sum_ref[...])
            for n in range(len(peers) + 1):
                term = small_v[i]
                for m in range(1, len(peers) + 1):
                    term = jnp.where(mine == n ^ m, small_v[slot_of[i] + m - 1], term)
                total = total + term
            if i + 1 < stages:
                small_v[i + 1] = total
                return small_send(i + 1)
            sum_ref[...] = total

        tiny = small_send(0)
        sums.tick()
        sums.tick()
        tiny = small_add(0, tiny)
        sums.tick()
        tiny = small_add(1, tiny)
        out_scatter.finish()
        ends.append(pltpu.make_async_copy(ocore_v.at[0], dwout_hbm, sem.at[8]))
        ends[-1].start()
        for r in range(ex_size):
            result_copy(r).wait()
        load = pltpu.make_async_copy(ret_hbm, ret_v.at[pl.ds(0, slots)], sem.at[9])
        load.start()
        sums.tick()
        tiny = small_add(2, tiny)
        load.wait()
        for turn in range(2):
            def pick_one(n, _, turn=turn):
                at, one, two = place_tile(n)
                pick_v[:, at] = jnp.where((one, two)[turn], 1.0, 0.0).astype(low)
                return 0

            lax.fori_loop(0, padded // 128, pick_one, 0)

            def deliver(n, _, turn=turn):
                at = pl.ds(pl.multiple_of(n * 256, 256), 256)
                term = dot_nn(pick_v[...], ret_v[:, at]) * gates_ref[:, turn:turn + 1]
                if turn == 0:
                    g_v[:, at] = term
                else:
                    out_ref[:, at] = (mixed_v[:, at] + (g_v[:, at] + term)).astype(low)
                return 0

            lax.fori_loop(0, feat // 256, deliver, 0)
            if turn == 0:
                sums.tick()
                small_add(3, tiny)
        sums.finish()
        for copy in ends:
            copy.wait()

    rows, steps = 8 * feat, 13
    pl.run_scoped(
        backward, pltpu.VMEM((heads, count + half, half), low), pltpu.VMEM((count, 3 * feat), low),
        pltpu.VMEM((feat, count), low), pltpu.VMEM((feat, feat), low), pltpu.VMEM((count, 3 * feat), low),
        pltpu.VMEM((rows, wide), low),
        pltpu.VMEM((rows // 2, wide), low), pltpu.VMEM((count, feat), full), pltpu.VMEM((count, feat), full),
        pltpu.VMEM((count, padded), low), pltpu.VMEM((128, count), full), dma((steps,)))


def layer(tokens, cotangent, chosen, gates, lengths, keep, gain1, gain2, wqkv, wo, in_shard, out_shard, fin, fout, kinds, cap,
          dp_size, ex_size):
    count, feat = tokens.shape
    shard = in_shard.shape[0]
    hidden = dp_size * shard
    far, slots = dp_size // 2, kinds * cap
    padded = (slots + 127) // 128 * 128
    heads, half = feat // 64, count // 2
    rows, wide = 8 * feat, feat // 2
    span = 768 if ex_size * cap <= 1024 else 384
    steps = 2 * hidden // span
    chunks, stages = len(sum_chunks(dp_size, ex_size, rows)), 4
    anyspace, vmem = pl.BlockSpec(memory_space=pl.ANY), pl.BlockSpec(memory_space=pltpu.VMEM)
    dma, shape, buffer = pltpu.SemaphoreType.DMA, jax.ShapeDtypeStruct, pltpu.VMEM
    full, low = jnp.float32, jnp.bfloat16
    scatter = [buffer((far, shard, feat), low), buffer((far - 1, shard, feat), low), buffer((far - 1, shard, feat), low)]
    return pl.pallas_call(
        functools.partial(layer_kernel, dp_size, ex_size, kinds, cap),
        out_shape=(shape((count, feat), low), shape((count, feat), low), shape((rows, wide), low), shape((8, feat), full),
                   shape((shard, feat), low), shape((shard, feat), low),
                   shape((slots, feat), low), shape((slots, feat), low), shape((count, 3 * feat), low),
                   shape((heads, count + half, half), low), shape((feat, count), low), shape((feat, count), low)),
        in_specs=[pl.BlockSpec(memory_space=pltpu.SMEM)] + [vmem] * 8 + [anyspace] * 6,
        out_specs=(vmem, vmem, anyspace, vmem) + (anyspace,) * 8,
        scratch_shapes=[
            buffer((padded, feat), low), buffer((padded, feat), low),
            buffer((ex_size * cap, feat), low), buffer((ex_size * cap, feat), low),
            buffer((hidden, feat), low), buffer((hidden, feat), low)] + scatter + scatter + [
            buffer((rows, wide), low), buffer((count, feat), full), buffer((8, count), full), buffer((count, 8), full),
            buffer((24, feat), full), buffer((8, 128), full), buffer((4 * stages, 8, feat), full),
            dma((2, ex_size)), dma((2, ex_size)), dma((2, ex_size)), dma((2, ex_size)),
            dma((2, 2, far)), dma((2, 2, far)), dma((2, 2, far)), dma((2, 2, far)),
            dma((2, chunks, stages, 4)), dma((2, chunks, stages, 4)), dma((chunks,)),
            dma((2, stages, 4)), dma((3,)), dma((feat // 128,)),
        ],
        compiler_params=pltpu.CompilerParams(collective_id=0, has_side_effects=True, vmem_limit_bytes=63 << 20),
        name="layer",
    )(lengths, chosen.T, gates.T, keep[None], gates, tokens, cotangent, gain1, gain2, wqkv, wo, in_shard, out_shard,
      fin.reshape(steps, span, feat), fout.reshape(steps, span, feat))


def finish_kernel(kinds, total_hbm, small_ref, out_in, dtok_in, dwin_in, dwout_in,
                  out_ref, dtok_ref, gain1_ref, qkv_hbm, wide_hbm, gain2_ref, dwin_ref, dwout_ref, count_ref,
                  block_v, whole_v, load_sem, store_sem):
    feat = small_ref.shape[1]
    wide = feat // 2
    loads = [pltpu.make_async_copy(total_hbm.at[pl.ds(b * feat, feat)], block_v.at[b], load_sem.at[b]) for b in range(8)]
    for copy in loads:
        copy.start()
    out_ref[...] = out_in[...]
    dtok_ref[...] = dtok_in[...]
    stores = []
    for b in range(8):
        loads[b].wait()

        def widen(j, _):
            at = pl.ds(pl.multiple_of(j * 64, 64), 64)
            whole_v[b, at, :] = block_v[b, at, :].astype(jnp.float32)
            return 0

        lax.fori_loop(0, feat // 64, widen, 0)
        part, c = (b - 2) // 3, (b - 2) % 3
        target = wide_hbm.at[:, pl.ds(b * wide, wide)] if b < 2 else qkv_hbm.at[:, pl.ds(c * feat + part * wide, wide)]
        stores.append(pltpu.make_async_copy(whole_v.at[b], target, store_sem.at[b]))
        stores[-1].start()
    for source, target in ((dwin_in, dwin_ref), (dwout_in, dwout_ref)):
        def widen(j, _):
            at = pl.ds(pl.multiple_of(j * 64, 64), 64)
            target[at, :] = source[at, :].astype(jnp.float32)
            return 0

        lax.fori_loop(0, source.shape[0] // 64, widen, 0)
    gain1_ref[...] = small_ref[0, :]
    gain2_ref[...] = small_ref[1, :]
    count_ref[...] = small_ref[2, 0:128]
    for copy in stores:
        copy.wait()


def finish(total, small, out, dtok, dwin, dwout, kinds):
    rows, wide = total.shape
    feat = 2 * wide
    anyspace, vmem = pl.BlockSpec(memory_space=pl.ANY), pl.BlockSpec(memory_space=pltpu.VMEM)
    shape, full, low = jax.ShapeDtypeStruct, jnp.float32, jnp.bfloat16
    return pl.pallas_call(
        functools.partial(finish_kernel, kinds),
        out_shape=(shape(out.shape, low), shape(dtok.shape, low), shape((feat,), full), shape((feat, 3 * feat), full),
                   shape((feat, feat), full), shape((feat,), full), shape(dwin.shape, full), shape(dwout.shape, full),
                   shape((128,), full)),
        in_specs=[anyspace] + [vmem] * 5,
        out_specs=(vmem, vmem, vmem, anyspace, anyspace, vmem, vmem, vmem, vmem),
        scratch_shapes=[pltpu.VMEM((8, feat, wide), low), pltpu.VMEM((8, feat, wide), full),
                        pltpu.SemaphoreType.DMA((8,)), pltpu.SemaphoreType.DMA((8,))],
        compiler_params=pltpu.CompilerParams(vmem_limit_bytes=48 << 20),
        name="finish",
    )(total, small, out, dtok, dwin, dwout)


FROZEN = 2


def body(
    tokens,
    cotangent,
    chosen,
    gates,
    lengths,
    keep_mask,
    gain1,
    w_qkv,
    w_o,
    gain2,
    frozen_in,
    frozen_out,
    w_in,
    w_out,
):
    row_count, feat_width = tokens.shape
    owners = lax.axis_size("expert")
    dp_size = lax.axis_size("dp")
    kind_count = FROZEN + owners
    slot_count = ((2 * row_count * 5 // (4 * kind_count) + 7) // 8 * 8 + 15) // 16 * 16
    output, tokens_grad, total, small_sum, d_w_in, d_w_out = layer(
        tokens, cotangent, chosen, gates, lengths, keep_mask, gain1, gain2, w_qkv, w_o, w_in[0], w_out[0], frozen_in,
        frozen_out, kind_count, slot_count, dp_size, owners)[:6]
    output, tokens_grad, gain1_sum, w_qkv_sum, w_o_sum, gain2_sum, d_w_in, d_w_out, counts = finish(
        total, small_sum, output, tokens_grad, d_w_in, d_w_out, kind_count)
    return (
        output,
        tokens_grad,
        gain1_sum,
        w_qkv_sum,
        w_o_sum,
        gain2_sum,
        d_w_in[None],
        d_w_out[None],
        counts[:kind_count],
    )


def solution(mesh):
    placed = (
        P(("dp", "expert"), None),
        P(("dp", "expert"), None),
        P(("dp", "expert"), None),
        P(("dp", "expert"), None),
        P(("dp", "expert"), None),
        P(("dp", "expert")),
        P(),
        P(),
        P(),
        P(),
        P(),
        P(),
        P("expert", "dp", None),
        P("expert", "dp", None),
    )
    return jax.shard_map(
        body,
        mesh=mesh,
        in_specs=placed,
        out_specs=(
            P(("dp", "expert"), None),
            P(("dp", "expert"), None),
            P(),
            P(),
            P(),
            P(),
            P("expert", "dp", None),
            P("expert", "dp", None),
            P(),
        ),
        check_vma=False,
    )
```

time: 612 us -> 230 us (0.38); the launches traced: 602 us -> 229 us
  Pallas kernels: 0 us -> 221 us
  waiting for transfers between devices: 194 us -> 0 us
  matrix products: 142 us -> 0 us
  local copies, waits for them, and re-layouts: 107 us -> 7.08 us
  other arithmetic: 83.4 us -> 0 us
  blocking collectives: 40.2 us -> 0 us
  starting transfers between devices: 20.8 us -> 0 us
  between operations: 14.9 us -> 0.84 us
    pallas_call x0 -> x2, Pallas kernels: none -> 221 us  [the longest x1 213 us: layer(): pl.pallas_call(functools.partial(layer_kernel, dp_size, ex_size, kinds, c...]
    dot_general x21 -> x0, matrix products: 142 us -> none  [the longest x2 20 us: expert_forward(): jnp.einsum('gcf,gfd->gcd', active, down_weights, preferred_element_type=j...]
    psum x1 -> x0, waiting for transfers between devices: 129 us -> none  [body(): lax.psum((gain1_grad, w_qkv_grad, w_o_grad, gain2_grad, local_counts), ('...]
    all_to_all x4 -> x0, waiting for transfers between devices: 63.5 us -> none  [the longest x1 26.3 us: body(): lax.all_to_all(routed_grad, 'expert', split_axis=0, concat_axis=0, tiled=...]
    psum x1 -> x0, blocking collectives: 40.2 us -> none  [body(): lax.psum((gain1_grad, w_qkv_grad, w_o_grad, gain2_grad, local_counts), ('...]
    reduce_sum x11 -> x0, other arithmetic: 38 us -> none  [the longest x1 16.3 us: body(): output = mixed_rows + jnp.sum(picked * gates[:, :, None], axis=1)]
    all_to_all x4 -> x0, starting transfers between devices: 20.7 us -> none  [the longest x1 7.33 us: body(): lax.all_to_all(routed_rows, 'expert', split_axis=0, concat_axis=0, tiled=...]
    slice x10 -> x0, local copies, waits for them, and re-layouts: 20.6 us -> none  [the longest x2 5.4 us: body(): projected[:, feat_width:2 * feat_width].reshape(row_count, HEADS, HEAD_DIM)]
  transfers between devices with their start and end apart: 8 -> 0, of which waited for: 5 -> 0; matrix products, arithmetic and copies ran while one was open for 48% -> 0% of each run, Pallas kernels for 0% -> 0%
where the time goes in v1:
time: 230 us; the launch traced here: 229 us
  Pallas kernels  221 us (96%)
  local copies, waits for them, and re-layouts  7.08 us (3%)
    pallas_call x1, Pallas kernels, layer(): pl.pallas_call(functools.partial(layer_kernel, dp_size, ex_size, kinds, c...  213 us
    pallas_call x1, Pallas kernels, finish(): pl.pallas_call(functools.partial(finish_kernel, kinds), out_shape=(shape(...  7.66 us
    unnamed x11, local copies, waits for them, and re-layouts  7.08 us

profile of v1, /device:TPU:0, one launch (start us, length us, event | category | flops | bytes accessed | tf_op | source)
XLA Modules:
  0.0 228.7 jit_solution(1237570166962229169)
XLA Ops:
  0.6 1.5 copy.23.gates_ref
  2.2 213.1 %layer.1 = (bf16[512,768]{1,0:T(8,128)(2,1)}, bf16[512,768]{1,0:T(8,128)(2,1)}, bf16[6144,384]{1,0:T(8,128)(2,1)}, f32[8,768]{1,0:T(8,128)}, bf16[768,768]{1,0:T...) custom-call(s32[1,8]{1,0:T(1,128)} %lengths_s.1, ...), custom_call_target="tpu_custom_call" | custom-call | tf_op jit(solution)/shard_map/layer/pallas_call | solution.py:842
  215.3 0.0 copy-start
  215.3 1.3 copy-done
  216.6 0.0 copy-start.1
  216.6 1.3 copy-done.1
  217.9 0.0 copy-start.2
  217.9 1.1 copy-done.2
  219.0 0.0 copy-start.3
  219.0 1.1 copy-done.3
  220.1 0.0 copy-start.4
  220.1 0.7 copy-done.4
  220.9 7.7 %finish.1 = (bf16[512,768]{1,0:T(8,128)(2,1)}, bf16[512,768]{1,0:T(8,128)(2,1)}, f32[768]{0:T(1024)}, f32[768,2304]{1,0:T(8,128)}, f32[768,768]{1,0:T(8,128)}, /...) custom-call(bf16[6144,384]{1,0:T(8,128)(2,1)} %get-tuple-element.24.total_hbm, ...), custom_call_target="tpu_custom_call" | custom-call | tf_op jit(solution)/shard_map/finish/pallas_call | solution.py:910
Async XLA Ops:
  215.3 1.3 copy-start
  216.6 1.3 copy-start.1
  217.9 1.1 copy-start.2
  219.0 1.1 copy-start.3
  220.1 0.7 copy-start.4

commit v2 on v1

--- a/solution.py
+++ b/solution.py
@@ -244,20 +244,22 @@
 
     def finish(self):
         while any(self.copies):
-            self.tick()
+            for c in range(len(self.chunks)):
+                self.advance(c)
 
 
 def sum_chunks(dp_size, ex_size, rows):
     core, xs, ys, zs = butterfly(dp_size, ex_size)
     yxz, xyz, zyx = [[core], ys, xs, zs], [[core], xs, ys, zs], [[core], zs, ys, xs]
     if dp_size * ex_size * 16 <= 512:
-        return [(0, 1536, yxz, 0), (1536, 2048, yxz, 1), (3584, 1024, yxz, 2), (4608, 1024, xyz, 2), (5632, 512, zyx, 2)]
+        yq, xq, zq = [[core], ys, xs + zs[:1], zs[1:]], [[core], xs, ys + zs[:1], zs[1:]], [[core], zs[:1], ys + xs, zs[1:]]
+        return [(0, 1536, yq, 0), (1536, 1024, xq, 1), (2560, 1024, yq, 1), (3584, 1024, yq, 2), (4608, 1024, xq, 2), (5632, 512, zq, 2)]
     third = rows // 3
     return [(0, third, yxz, 2), (third, third, xyz, 2), (2 * third, third, zyx, 2)]
 
 
 def layer_kernel(dp_size, ex_size, kinds, cap,
-                 lengths_s, chosen_ref, gatest_ref, keep_ref, gates_ref, tok_ref, cot_ref, gain1_ref, gain2_ref,
+                 lengths_s, chosen_ref, gatest_ref, keep_ref, tok_ref, cot_ref, gain1_ref, gain2_ref,
                  wqkv_hbm, wo_hbm, in_hbm, outw_hbm, fin_hbm, fout_hbm,
                  out_ref, dtok_ref, total_hbm, sum_ref, dwin_hbm, dwout_hbm,
                  back_hbm, ret_hbm, proj_hbm, prob_hbm, attt_hbm, normt_hbm,
@@ -359,7 +361,8 @@
                 end = end + lengths_s[0, j]
         place_v[2:3, :] = document
         place_v[3:4, :] = keep_ref[...].astype(full)
-        place_v[4:8, :] = jnp.zeros((4, count), full)
+        place_v[4:6, :] = gatest_ref[...]
+        place_v[6:8, :] = jnp.zeros((2, count), full)
         columns = place_v[...].T
         column_v[...] = columns
 
@@ -459,7 +462,7 @@
         pltpu.VMEM((feat, count), low), pltpu.VMEM((count, 3 * feat), low), pltpu.VMEM((heads, count + half, half), low),
         pltpu.VMEM((feat, count), low), pltpu.VMEM((count, feat), low), pltpu.VMEM((count, count), full), dma((5,)))
 
-    def expert(act_v, hg_v, fin_v, fout_v, facc_v, fst_v, rg_v, sem, load_sem):
+    def expert(act_v, hg_v, fin_v, fout_v, facc_v, fst_v, rg_v, even_v, odd_v, sem, load_sem):
         steps = fin_hbm.shape[0]
         per = steps // 2
 
@@ -534,14 +537,28 @@
                 if r:
                     row_copy(r).wait_recv()
 
-            def hidden_tile(t, _, here=here):
+            size = pl.ds(0, len(group) * cap)
+
+            def units(t, target, here=here, size=size):
                 at = pl.ds(pl.multiple_of(t * 256, 256), 256)
-                active, slope = gelu_pair(dot_nt(rows_v[here, :], win_v[at, :]))
+                target[size, :] = dot_nt(rows_v[here, :], win_v[at, :])
+
+            def gelu_tile(t, source, here=here, size=size):
+                at = pl.ds(pl.multiple_of(t * 256, 256), 256)
+                active, slope = gelu_pair(source[size, :])
                 act_v[here, at] = active.astype(low)
                 hg_v[here, at] = (hg_v[here, at].astype(full) * slope).astype(low)
+
+            units(0, even_v)
+
+            def tile_pair(i, _):
+                units(2 * i + 1, odd_v)
+                gelu_tile(2 * i, even_v)
+                units(lax.rem(2 * i + 2, tiles), even_v)
+                gelu_tile(2 * i + 1, odd_v)
                 return 0
 
-            lax.fori_loop(0, tiles, hidden_tile, 0)
+            lax.fori_loop(0, tiles // 2, tile_pair, 0)
 
             def back_tile(n, _, here=here):
                 at = pl.ds(pl.multiple_of(n * 256, 256), 256)
@@ -595,7 +612,8 @@
     pl.run_scoped(
         expert, pltpu.VMEM((rows_all, hidden), low), pltpu.VMEM((rows_all, hidden), low), pltpu.VMEM((2, span, feat), low),
         pltpu.VMEM((2, span, feat), low), pltpu.VMEM((2, 2, cap, feat), full), pltpu.VMEM((2, 2 * cap, feat), low),
-        pltpu.VMEM((rows_all, feat), low), dma((3,)), dma((2, 2)))
+        pltpu.VMEM((rows_all, feat), low), pltpu.VMEM((rows_all // 2, 256), full), pltpu.VMEM((rows_all // 2, 256), full),
+        dma((3,)), dma((2, 2)))
 
     back_v, ret_v, branch_v, da_v = grad_st, token_st, grad_v.at[pl.ds(0, count)], grad_v.at[pl.ds(count, count)]
 
@@ -743,7 +761,8 @@
 
         lax.fori_loop(0, count // 64, first_norm, 0)
 
-        order = sums.chunks[0][2]
+        core, xs, ys, zs = butterfly(dp_size, ex_size)
+        order = [[core], ys, xs, zs]
         stages = len(order)
         slot_of = [stages + sum((1 << len(stage)) - 1 for stage in order[:i]) for i in range(stages)]
         for i in range(3):
@@ -799,7 +818,7 @@
 
             def deliver(n, _, turn=turn):
                 at = pl.ds(pl.multiple_of(n * 256, 256), 256)
-                term = dot_nn(pick_v[...], ret_v[:, at]) * gates_ref[:, turn:turn + 1]
+                term = dot_nn(pick_v[...], ret_v[:, at]) * column_v[:, 4 + turn:5 + turn]
                 if turn == 0:
                     g_v[:, at] = term
                 else:
@@ -845,7 +864,7 @@
                    shape((shard, feat), low), shape((shard, feat), low),
                    shape((slots, feat), low), shape((slots, feat), low), shape((count, 3 * feat), low),
                    shape((heads, count + half, half), low), shape((feat, count), low), shape((feat, count), low)),
-        in_specs=[pl.BlockSpec(memory_space=pltpu.SMEM)] + [vmem] * 8 + [anyspace] * 6,
+        in_specs=[pl.BlockSpec(memory_space=pltpu.SMEM)] + [vmem] * 7 + [anyspace] * 6,
         out_specs=(vmem, vmem, anyspace, vmem) + (anyspace,) * 8,
         scratch_shapes=[
             buffer((padded, feat), low), buffer((padded, feat), low),
@@ -860,63 +879,73 @@
         ],
         compiler_params=pltpu.CompilerParams(collective_id=0, has_side_effects=True, vmem_limit_bytes=63 << 20),
         name="layer",
-    )(lengths, chosen.T, gates.T, keep[None], gates, tokens, cotangent, gain1, gain2, wqkv, wo, in_shard, out_shard,
+    )(lengths, chosen.T, gates.T, keep[None], tokens, cotangent, gain1, gain2, wqkv, wo, in_shard, out_shard,
       fin.reshape(steps, span, feat), fout.reshape(steps, span, feat))
 
 
-def finish_kernel(kinds, total_hbm, small_ref, out_in, dtok_in, dwin_in, dwout_in,
-                  out_ref, dtok_ref, gain1_ref, qkv_hbm, wide_hbm, gain2_ref, dwin_ref, dwout_ref, count_ref,
-                  block_v, whole_v, load_sem, store_sem):
-    feat = small_ref.shape[1]
+def finish_kernel(total_hbm, small_hbm, out_in, dtok_in, dwin_in, dwout_in,
+                  out_hbm, dtok_hbm, gain1_ref, qkv_hbm, wide_hbm, gain2_ref, dwin_hbm, dwout_hbm, count_ref,
+                  block_v, whole_v, shard_v, shard_w, row_v, small_v, load_sem, store_sem):
+    feat = small_v.shape[1]
     wide = feat // 2
-    loads = [pltpu.make_async_copy(total_hbm.at[pl.ds(b * feat, feat)], block_v.at[b], load_sem.at[b]) for b in range(8)]
-    for copy in loads:
-        copy.start()
-    out_ref[...] = out_in[...]
-    dtok_ref[...] = dtok_in[...]
+    copy = pltpu.make_async_copy
+    loads = [copy(total_hbm.at[pl.ds(b * feat, feat)], block_v.at[b], load_sem.at[b]) for b in range(8)]
+    loads += [copy(source, shard_v.at[n], load_sem.at[8 + n]) for n, source in enumerate((dwin_in, dwout_in))]
+    loads += [copy(source, row_v.at[n], load_sem.at[10 + n]) for n, source in enumerate((out_in, dtok_in))]
+    loads.append(copy(small_hbm, small_v, load_sem.at[12]))
+    for load in loads:
+        load.start()
     stores = []
+
+    def widen(source, target, rows):
+        def tile(j, _):
+            at = pl.ds(pl.multiple_of(j * 64, 64), 64)
+            target[at, :] = source[at, :].astype(jnp.float32)
+            return 0
+
+        lax.fori_loop(0, rows // 64, tile, 0)
+
+    def store(source, target):
+        stores.append(copy(source, target, store_sem.at[len(stores)]))
+        stores[-1].start()
+
     for b in range(8):
         loads[b].wait()
-
-        def widen(j, _):
-            at = pl.ds(pl.multiple_of(j * 64, 64), 64)
-            whole_v[b, at, :] = block_v[b, at, :].astype(jnp.float32)
-            return 0
-
-        lax.fori_loop(0, feat // 64, widen, 0)
+        widen(block_v.at[b], whole_v.at[b], feat)
         part, c = (b - 2) // 3, (b - 2) % 3
-        target = wide_hbm.at[:, pl.ds(b * wide, wide)] if b < 2 else qkv_hbm.at[:, pl.ds(c * feat + part * wide, wide)]
-        stores.append(pltpu.make_async_copy(whole_v.at[b], target, store_sem.at[b]))
-        stores[-1].start()
-    for source, target in ((dwin_in, dwin_ref), (dwout_in, dwout_ref)):
-        def widen(j, _):
-            at = pl.ds(pl.multiple_of(j * 64, 64), 64)
-            target[at, :] = source[at, :].astype(jnp.float32)
-            return 0
-
-        lax.fori_loop(0, source.shape[0] // 64, widen, 0)
-    gain1_ref[...] = small_ref[0, :]
-    gain2_ref[...] = small_ref[1, :]
-    count_ref[...] = small_ref[2, 0:128]
-    for copy in stores:
-        copy.wait()
-
-
-def finish(total, small, out, dtok, dwin, dwout, kinds):
+        store(whole_v.at[b],
+              wide_hbm.at[:, pl.ds(b * wide, wide)] if b < 2 else qkv_hbm.at[:, pl.ds(c * feat + part * wide, wide)])
+    for n, target in enumerate((dwin_hbm, dwout_hbm)):
+        loads[8 + n].wait()
+        widen(shard_v.at[n], shard_w.at[n], shard_v.shape[1])
+        store(shard_w.at[n], target)
+    for n, target in enumerate((out_hbm, dtok_hbm)):
+        loads[10 + n].wait()
+        store(row_v.at[n], target)
+    loads[12].wait()
+    gain1_ref[...] = small_v[0, :]
+    gain2_ref[...] = small_v[1, :]
+    count_ref[...] = small_v[2, 0:128]
+    for load in stores:
+        load.wait()
+
+
+def finish(total, small, out, dtok, dwin, dwout):
     rows, wide = total.shape
     feat = 2 * wide
     anyspace, vmem = pl.BlockSpec(memory_space=pl.ANY), pl.BlockSpec(memory_space=pltpu.VMEM)
-    shape, full, low = jax.ShapeDtypeStruct, jnp.float32, jnp.bfloat16
+    shape, full, low, buffer = jax.ShapeDtypeStruct, jnp.float32, jnp.bfloat16, pltpu.VMEM
     return pl.pallas_call(
-        functools.partial(finish_kernel, kinds),
+        finish_kernel,
         out_shape=(shape(out.shape, low), shape(dtok.shape, low), shape((feat,), full), shape((feat, 3 * feat), full),
                    shape((feat, feat), full), shape((feat,), full), shape(dwin.shape, full), shape(dwout.shape, full),
                    shape((128,), full)),
-        in_specs=[anyspace] + [vmem] * 5,
-        out_specs=(vmem, vmem, vmem, anyspace, anyspace, vmem, vmem, vmem, vmem),
-        scratch_shapes=[pltpu.VMEM((8, feat, wide), low), pltpu.VMEM((8, feat, wide), full),
-                        pltpu.SemaphoreType.DMA((8,)), pltpu.SemaphoreType.DMA((8,))],
-        compiler_params=pltpu.CompilerParams(vmem_limit_bytes=48 << 20),
+        in_specs=[anyspace] * 6,
+        out_specs=(anyspace, anyspace, vmem, anyspace, anyspace, vmem, anyspace, anyspace, vmem),
+        scratch_shapes=[buffer((8, feat, wide), low), buffer((8, feat, wide), full), buffer((2,) + dwin.shape, low),
+                        buffer((2,) + dwin.shape, full), buffer((2,) + out.shape, low), buffer(small.shape, full),
+                        pltpu.SemaphoreType.DMA((13,)), pltpu.SemaphoreType.DMA((12,))],
+        compiler_params=pltpu.CompilerParams(vmem_limit_bytes=63 << 20),
         name="finish",
     )(total, small, out, dtok, dwin, dwout)
 
@@ -949,7 +978,7 @@
         tokens, cotangent, chosen, gates, lengths, keep_mask, gain1, gain2, w_qkv, w_o, w_in[0], w_out[0], frozen_in,
         frozen_out, kind_count, slot_count, dp_size, owners)[:6]
     output, tokens_grad, gain1_sum, w_qkv_sum, w_o_sum, gain2_sum, d_w_in, d_w_out, counts = finish(
-        total, small_sum, output, tokens_grad, d_w_in, d_w_out, kind_count)
+        total, small_sum, output, tokens_grad, d_w_in, d_w_out)
     return (
         output,
         tokens_grad,

time: 230 us -> 219 us (0.952)
  local copies, waits for them, and re-layouts: 7.08 us -> 0 us
  Pallas kernels: 221 us -> 218 us
    unnamed x11 -> x0, local copies, waits for them, and re-layouts: 7.08 us -> none
    pallas_call x1, Pallas kernels: 213 us -> 209 us  [layer(): pl.pallas_call(functools.partial(layer_kernel, dp_size, ex_size, kinds, c...]
where the time goes in v2:
time: 219 us; the launch traced here: 218 us
  Pallas kernels  218 us (100%)
    pallas_call x1, Pallas kernels, layer(): pl.pallas_call(functools.partial(layer_kernel, dp_size, ex_size, kinds, c...  209 us
    pallas_call x1, Pallas kernels, finish(): pl.pallas_call(finish_kernel, out_shape=(shape(out.shape, low), shape(dto...  8.53 us

profile of v2, /device:TPU:0, one launch (start us, length us, event | category | flops | bytes accessed | tf_op | source)
XLA Modules:
  0.0 218.4 jit_solution(715675253533595319)
XLA Ops:
  0.6 209.0 %layer.1 = (bf16[512,768]{1,0:T(8,128)(2,1)}, bf16[512,768]{1,0:T(8,128)(2,1)}, bf16[6144,384]{1,0:T(8,128)(2,1)}, f32[8,768]{1,0:T(8,128)}, bf16[768,768]{1,0:T...) custom-call(s32[1,8]{1,0:T(1,128)} %lengths_s.1, ...), custom_call_target="tpu_custom_call" | custom-call | tf_op jit(solution)/shard_map/layer/pallas_call | solution.py:861
  209.7 8.5 %finish.1 = (bf16[512,768]{1,0:T(8,128)(2,1)}, bf16[512,768]{1,0:T(8,128)(2,1)}, f32[768]{0:T(1024)}, f32[768,2304]{1,0:T(8,128)}, f32[768,768]{1,0:T(8,128)}, /...) custom-call(bf16[6144,384]{1,0:T(8,128)(2,1)} %get-tuple-element.24.total_hbm, ...), custom_call_target="tpu_custom_call" | custom-call | tf_op jit(solution)/shard_map/finish/pallas_call | solution.py:938

commit v3 on v2

--- a/solution.py
+++ b/solution.py
@@ -599,9 +599,9 @@
             return 0
 
         lax.fori_loop(0, feat // 256, result_tile, 0)
+        all_shards(out_scatter, act_v, grad_v)
         for r in reversed(range(ex_size)):
             result_copy(r).start()
-        all_shards(out_scatter, act_v, grad_v)
         for copy in stores:
             copy.wait()
         for r in range(ex_size):
@@ -796,8 +796,6 @@
         sums.tick()
         sums.tick()
         tiny = small_add(0, tiny)
-        sums.tick()
-        tiny = small_add(1, tiny)
         out_scatter.finish()
         ends.append(pltpu.make_async_copy(ocore_v.at[0], dwout_hbm, sem.at[8]))
         ends[-1].start()
@@ -806,7 +804,7 @@
         load = pltpu.make_async_copy(ret_hbm, ret_v.at[pl.ds(0, slots)], sem.at[9])
         load.start()
         sums.tick()
-        tiny = small_add(2, tiny)
+        tiny = small_add(1, tiny)
         load.wait()
         for turn in range(2):
             def pick_one(n, _, turn=turn):
@@ -826,9 +824,8 @@
                 return 0
 
             lax.fori_loop(0, feat // 256, deliver, 0)
-            if turn == 0:
-                sums.tick()
-                small_add(3, tiny)
+            sums.tick()
+            tiny = small_add(2 + turn, tiny)
         sums.finish()
         for copy in ends:
             copy.wait()

time: 219 us -> 218 us (level)
  no operation moved by 1% of the time
where the time goes in v3:
time: 218 us; the launch traced here: 217 us
  Pallas kernels  216 us (99%)
    pallas_call x1, Pallas kernels, layer(): pl.pallas_call(functools.partial(layer_kernel, dp_size, ex_size, kinds, c...  208 us
    pallas_call x1, Pallas kernels, finish(): pl.pallas_call(finish_kernel, out_shape=(shape(out.shape, low), shape(dto...  8.53 us

profile of v3, /device:TPU:0, one launch (start us, length us, event | category | flops | bytes accessed | tf_op | source)
XLA Modules:
  0.0 217.1 jit_solution(16300387148068760964)
XLA Ops:
  0.6 207.7 %layer.1 = (bf16[512,768]{1,0:T(8,128)(2,1)}, bf16[512,768]{1,0:T(8,128)(2,1)}, bf16[6144,384]{1,0:T(8,128)(2,1)}, f32[8,768]{1,0:T(8,128)}, bf16[768,768]{1,0:T...) custom-call(s32[1,8]{1,0:T(1,128)} %lengths_s.1, ...), custom_call_target="tpu_custom_call" | custom-call | tf_op jit(solution)/shard_map/layer/pallas_call | solution.py:858
  208.4 8.5 %finish.1 = (bf16[512,768]{1,0:T(8,128)(2,1)}, bf16[512,768]{1,0:T(8,128)(2,1)}, f32[768]{0:T(1024)}, f32[768,2304]{1,0:T(8,128)}, f32[768,768]{1,0:T(8,128)}, /...) custom-call(bf16[6144,384]{1,0:T(8,128)(2,1)} %get-tuple-element.24.total_hbm, ...), custom_call_target="tpu_custom_call" | custom-call | tf_op jit(solution)/shard_map/finish/pallas_call | solution.py:935
